TPU v7x, 256 devices: a whole 4x4x8 slice. The times are simulated.
256 devices in a mesh: wide: 64 (over x, z, y_lo), half: 4 (over y_hi, core).
Axes of the slice: x: 4, y: 4 (y_hi: 2, y_lo: 2; y = y_hi * 2 + y_lo), z: 8, core: 2. Of those that a mesh axis runs over, the one named last changes fastest.
Arguments:
- focus: bfloat16 [128, 3072, 512], P('half', 'wide'), may hold values from -6 to 6
- kernel: bfloat16 [64, 2, 3072, 3072], P('wide', None, 'half'), may hold values from -0.1875 to 0.1875
- onset: int32 [128], replicated, may hold values from 128 to 511
- tile_mask: int32 [12, 12], replicated, may hold values 0 or 1
Outputs:
- updated: bfloat16 [128, 3072, 512], P('half', 'wide')
Inputs may be any that keep to these rules, and one draw needn't show every extreme that they name: `tile_mask`: 1 keeps a 256 x 256 block of the kernel, 0 removes it. Samples at and after the onset are muted.
All inputs are finite; a program needn't handle non-finite values.
Results may differ from a plain program's by a relative error of at most 0.012.
Values may be sent and summed in bfloat16 or wider, within the bound.
A program may use at most 128 MiB of HBM per device.

v0:
```python
import math

import jax
import jax.numpy as jnp
from jax import lax
from jax.sharding import PartitionSpec as P

TILE = 256


def from_everyone(array, axis):
    copies = jnp.broadcast_to(array, (lax.axis_size(axis), *array.shape))
    return lax.all_to_all(copies, axis, split_axis=0, concat_axis=0, tiled=True)


def joined_along(blocks, dim):
    blocks = jnp.moveaxis(blocks, 0, dim)
    shape = blocks.shape
    return blocks.reshape(*shape[:dim], shape[dim] * shape[dim + 1], *shape[dim + 2 :])


def collect(array, axis, dim):
    blocks = from_everyone(array, axis)
    return joined_along(blocks, dim)


def split_up(array, dim, devices):
    before, after = (array.shape[:dim], array.shape[dim + 1 :])
    return jnp.moveaxis(array.reshape(*before, devices, -1, *after), dim, 0)


def sent_and_summed(array, axis, dim):
    devices = lax.axis_size(axis)
    blocks = lax.all_to_all(split_up(array, dim, devices), axis, 0, 0, tiled=True)
    return jnp.sum(blocks.astype(jnp.float32), axis=0)


def make_tables(bins, length):
    times = jnp.arange(length, dtype=jnp.int32)
    number = jnp.arange(bins, dtype=jnp.int32) + 1
    phase = (number[None, :] * times[:, None] % length).astype(jnp.float32) * (
        2.0 * math.pi / length
    )
    table = jnp.stack([jnp.cos(phase), -jnp.sin(phase)], axis=2).reshape(length, 2 * bins)
    inverse = (table.T * (2.0 / length)).astype(jnp.bfloat16)
    return (table.astype(jnp.bfloat16), inverse)


def masked_panel(kernel, tile_mask):
    freq_dev, _, panel_rows, receivers = kernel.shape
    row_blocks = panel_rows // TILE
    col_blocks = receivers // TILE
    keeps = lax.dynamic_slice_in_dim(
        tile_mask, lax.axis_index("half") * row_blocks, row_blocks, 0
    ).astype(jnp.bfloat16)
    shaped = (
        kernel.reshape(freq_dev, 2, row_blocks, TILE, col_blocks, TILE)
        * keeps[None, None, :, None, :, None]
    )
    return shaped.reshape(kernel.shape)


def to_freq(values):
    return lax.all_to_all(values, "wide", split_axis=1, concat_axis=2, tiled=True)


def to_time(values):
    return lax.all_to_all(values, "wide", split_axis=2, concat_axis=1, tiled=True)


def forward_waves(values, panel):
    count = values.shape[0]
    freq_dev = panel.shape[0]
    split = values.reshape(count, freq_dev, 2, values.shape[2])
    kernel_real = panel[:, 0]
    kernel_imag = panel[:, 1]
    real_part = jnp.einsum(
        "pfs,frs->pfr", split[:, :, 0], kernel_real, preferred_element_type=jnp.float32
    ) - jnp.einsum("pfs,frs->pfr", split[:, :, 1], kernel_imag, preferred_element_type=jnp.float32)
    imag_part = jnp.einsum(
        "pfs,frs->pfr", split[:, :, 1], kernel_real, preferred_element_type=jnp.float32
    ) + jnp.einsum("pfs,frs->pfr", split[:, :, 0], kernel_imag, preferred_element_type=jnp.float32)
    stacked = jnp.stack([real_part, imag_part], axis=2)
    return stacked.reshape(count, 2 * freq_dev, panel.shape[2]).astype(jnp.bfloat16)


def shards(focus, kernel, onset, tile_mask):
    own_points, local_receivers, length = focus.shape
    freq_dev = kernel.shape[0]
    bins = freq_dev * lax.axis_size("wide")
    forward_lookup_table, inverse_lookup_table = make_tables(bins, length)
    panel = masked_panel(kernel, tile_mask)
    spectra = jnp.einsum(
        "fag,gz->fza", focus, forward_lookup_table, preferred_element_type=jnp.float32
    ).astype(jnp.bfloat16)
    waves = forward_waves(collect(to_freq(spectra), "half", 0), panel)
    temporal_domain = to_time(waves)
    seismic_trace = jnp.einsum(
        "jda,dw->jaw", temporal_domain, inverse_lookup_table, preferred_element_type=jnp.float32
    )
    sample = jnp.arange(length, dtype=jnp.int32)
    muted_window = jnp.where(
        sample[None, None, :] < onset[:, None, None], seismic_trace, 0.0
    ).astype(jnp.bfloat16)
    again = jnp.einsum(
        "fag,gz->fza", muted_window, forward_lookup_table, preferred_element_type=jnp.float32
    ).astype(jnp.bfloat16)
    returned = to_freq(again)
    panel_rows = panel.shape[2]
    kernel_real = panel[:, 0]
    kernel_imag = panel[:, 1]
    count = own_points * lax.axis_size("half")
    rows = returned.reshape(count, freq_dev, 2, panel_rows)
    wave_real = rows[:, :, 0]
    wave_imag = rows[:, :, 1]
    real_part = jnp.einsum(
        "pfr,frs->pfs", wave_real, kernel_real, preferred_element_type=jnp.float32
    ) + jnp.einsum("pfr,frs->pfs", wave_imag, kernel_imag, preferred_element_type=jnp.float32)
    imag_part = jnp.einsum(
        "pfr,frs->pfs", wave_imag, kernel_real, preferred_element_type=jnp.float32
    ) - jnp.einsum("pfr,frs->pfs", wave_real, kernel_imag, preferred_element_type=jnp.float32)
    summed = sent_and_summed(
        jnp.stack([real_part, imag_part], axis=2)
        .reshape(count, 2 * freq_dev, panel.shape[3])
        .astype(jnp.bfloat16),
        "half",
        0,
    ).astype(jnp.bfloat16)
    backward_pass = to_time(summed)
    focusing_update = jnp.einsum(
        "jda,dw->jaw", backward_pass, inverse_lookup_table, preferred_element_type=jnp.float32
    )
    mine = lax.dynamic_slice_in_dim(onset, lax.axis_index("half") * own_points, own_points, 0)
    kept = jnp.where(sample[None, None, :] < mine[:, None, None], focusing_update, 0.0)
    return (focus.astype(jnp.float32) + kept).astype(jnp.bfloat16)


def solution(mesh):
    in_specs = (P("half", "wide", None), P("wide", None, "half", None), P(), P())
    out_specs = P("half", "wide", None)
    return jax.shard_map(shards, mesh=mesh, in_specs=in_specs, out_specs=out_specs, check_vma=False)
```

profile of v0, /device:TPU:1, one launch (start us, length us, event | category | flops | bytes accessed | tf_op | source)
XLA Modules:
  0.0 189.6 jit_solution(7071183743135213570)
XLA Ops:
  0.8 2.0 %fusion.11 = bf16[32,128,48]{1,2,0:T(8,128)(2,1)S(1)} fusion(bf16[32,48,512]{2,1,0:T(8,128)(2,1)} %param.4, bf16[512,128]{0,1:T(8,128)(2,1)S(1)} %convert_element_type.65), kind=kOutput, calls=%fused_computation.20 | convolution fusion | flops 201523200 | bytes 2097152 | tf_op jit(solution)/shard_map/fag,gz->fza/dot_general | solution.py:93
  2.8 1.4 copy.56
  4.3 2.5 %reshape.247 = bf16[64,2,1536]{2,1,0:T(2,128)(2,1)} reshape(bf16[128,32,48]{2,1,0:T(8,128)(2,1)S(1)} %bitcast.125) | data formatting | bytes 786432
  6.8 13.7 %all-to-all-start = ((bf16[64,2,1536]{2,1,0:T(2,128)(2,1)}), bf16[64,2,1536]{2,1,0:T(2,128)(2,1)S(1)}, u32[]{:S(2)}, u32[]{:S(2)}) async-start(bf16[64,2,1536]{2,1,0:T(2,128)(2,1)} %reshape.247), calls=%async_computation | async-start | bytes 786432 | tf_op jit(solution)/shard_map/all_to_all | solution.py:64
  21.6 5.4 %copy.84 = bf16[96,8,12,256]{3,1,2,0:T(8,128)(2,1)} copy(bf16[96,8,12,256]{3,2,1,0:T(8,128)(2,1)S(1)} %bitcast.121) | data formatting | bytes 9437184
  27.0 6.4 %all-to-all-done = bf16[64,2,1536]{2,1,0:T(2,128)(2,1)S(1)} async-done(((bf16[64,2,1536]{2,1,0:T(2,128)(2,1)}), bf16[64,2,1536]{2,1,0:T(2,128)(2,1)S(1)}, u32[]{:S(2)}, u32[]{:S(2)}) %all-to-all-start) | async-done | bytes 393248 | tf_op jit(solution)/shard_map/all_to_all | solution.py:64
  35.1 2.0 %all_to_all.59 = bf16[32,2,3072]{2,0,1:T(8,128)(2,1)S(1)} reshape(bf16[32,2,64,48]{3,2,0,1:T(8,128)(2,1)S(1)} %copy.57) | data formatting | bytes 786432 | tf_op jit(solution)/shard_map/all_to_all | solution.py:64
  37.2 1.3 broadcast_in_dim.36
  38.5 7.0 %all-to-all-start.1 = ((bf16[4,32,2,3072]{3,1,2,0:T(8,128)(2,1)}), bf16[4,32,2,3072]{3,1,2,0:T(8,128)(2,1)S(1)}, u32[]{:S(2)}, u32[]{:S(2)}) async-start(bf16[4,32,2,3072]{3,1,2,0:T(8,128)(2,1)} %broadcast_in_dim.36), calls=%async_computation.1 | async-start | bytes 3145728 | tf_op jit(solution)/shard_map/all_to_all | solution.py:13
  45.5 8.7 %broadcast_multiply_fusion = bf16[1,2,768,3072]{3,2,1,0:T(8,128)(2,1)} fusion(bf16[1,2,768,3072]{3,2,1,0:T(8,128)(2,1)} %param.5, bf16[768,3072]{1,0:T(8,128)(2,1)} %bitcast.122), kind=kLoop, calls=%fused_computation.2 | loop fusion | flops 4718592 | bytes 23592960 | tf_op jit(solution)/shard_map/mul | solution.py:57
  54.2 11.9 %all-to-all-done.1 = bf16[4,32,2,3072]{3,1,2,0:T(8,128)(2,1)S(1)} async-done(((bf16[4,32,2,3072]{3,1,2,0:T(8,128)(2,1)}), bf16[4,32,2,3072]{3,1,2,0:T(8,128)(2,1)S(1)}, u32[]{:S(2)}, u32[]{:S(2)}) %all-to-all-start.1) | async-done | bytes 1572896 | tf_op jit(solution)/shard_map/all_to_all | solution.py:13
  66.2 3.9 %fusion.5 = f32[768,128]{1,0:T(8,128)S(1)} fusion(bf16[1,2,768,3072]{3,2,1,0:T(8,128)(2,1)} %broadcast_multiply_fusion, bf16[128,1,2,3072]{3,0,2,1:T(8,128)(2,1)S(1)} %bitcast.132), kind=kOutput, calls=%fused_computation.12 | convolution fusion | flops 603979776 | bytes 5898240 | tf_op jit(solution)/shard_map/pfs,frs->pfr/dot_general | solution.py:77
  70.1 1.2 copy-done
  71.3 1.4 fusion.4
  72.7 1.4 fusion.16
  74.1 1.4 fusion.17
  75.6 1.2 copy.59
  76.7 5.3 %all-to-all-start.2 = ((bf16[128,2,768]{0,1,2:T(2,128)(2,1)}), bf16[128,2,768]{0,1,2:T(2,128)(2,1)S(1)}, u32[]{:S(2)}, u32[]{:S(2)}) async-start(bf16[128,2,768]{0,1,2:T(2,128)(2,1)} %copy.59), calls=%async_computation.2 | async-start | bytes 786432 | tf_op jit(solution)/shard_map/all_to_all | solution.py:68
  82.5 12.8 %all-to-all-done.2 = bf16[128,2,768]{0,1,2:T(2,128)(2,1)S(1)} async-done(((bf16[128,2,768]{0,1,2:T(2,128)(2,1)}), bf16[128,2,768]{0,1,2:T(2,128)(2,1)S(1)}, u32[]{:S(2)}, u32[]{:S(2)}) %all-to-all-start.2) | async-done | bytes 393248 | tf_op jit(solution)/shard_map/all_to_all | solution.py:68
  95.6 1.0 fusion.10
  97.0 21.9 %all_to_all.79 = bf16[128,128,12]{0,2,1:T(8,128)(2,1)S(1)} all-to-all(bf16[128,128,12]{0,2,1:T(8,128)(2,1)S(1)} %copy.64), channel_id=1, replica_groups=mesh['wide'=64,'half'=4] {'wide'}, dimensions={1} | all-to-all | bytes 786432 | tf_op jit(solution)/shard_map/all_to_all | solution.py:64
  120.1 3.1 %fusion.2 = f32[3072,128]{0,1:T(8,128)S(1)} fusion(bf16[1,2,768,3072]{3,2,1,0:T(8,128)(2,1)} %broadcast_multiply_fusion, bf16[128,1,1,768]{3,0,2,1:T(8,128)(2,1)S(1)} %copy.66), kind=kOutput, calls=%fused_computation.9 | convolution fusion | flops 603979776 | bytes 6488064 | tf_op jit(solution)/shard_map/pfr,frs->pfs/dot_general | solution.py:116
  123.6 3.1 %fusion.3 = f32[3072,128]{0,1:T(8,128)S(1)} fusion(bf16[1,2,768,3072]{3,2,1,0:T(8,128)(2,1)} %broadcast_multiply_fusion, bf16[128,1,1,768]{3,0,2,1:T(8,128)(2,1)S(1)} %copy.67), kind=kOutput, calls=%fused_computation.10 | convolution fusion | flops 603979776 | bytes 6488064 | tf_op jit(solution)/shard_map/pfr,frs->pfs/dot_general | solution.py:119
  126.7 3.1 %fusion = bf16[3072,128]{0,1:T(8,128)(2,1)S(1)} fusion(f32[3072,128]{0,1:T(8,128)S(1)} %fusion.2, bf16[1,2,768,3072]{3,2,1,0:T(8,128)(2,1)} %broadcast_multiply_fusion, bf16[128,1,1,768]{3,0,2,1:T(8,128)(2,1)S(1)} %copy.67), kind=kOutput, calls=%fused_computation.5 | convolution fusion | flops 604766208 | bytes 7274496 | tf_op jit(solution)/shard_map/pfr,frs->pfs/dot_general | solution.py:118
  129.8 3.2 %fusion.1 = bf16[3072,128]{0,1:T(8,128)(2,1)S(1)} fusion(f32[3072,128]{0,1:T(8,128)S(1)} %fusion.3, bf16[1,2,768,3072]{3,2,1,0:T(8,128)(2,1)} %broadcast_multiply_fusion, bf16[128,1,1,768]{3,0,2,1:T(8,128)(2,1)S(1)} %copy.66), kind=kOutput, calls=%fused_computation.6 | convolution fusion | flops 604766208 | bytes 7274496 | tf_op jit(solution)/shard_map/pfr,frs->pfs/dot_general | solution.py:121
  133.2 26.5 %all_to_all.80 = bf16[4,32,2,3072]{3,1,2,0:T(8,128)(2,1)S(1)} all-to-all(bf16[4,32,2,3072]{3,1,2,0:T(8,128)(2,1)S(1)} %pad_maximum_fusion), channel_id=1, replica_groups=mesh['wide'=64,'half'=4] {'half'}, dimensions={0} | all-to-all | bytes 3145728 | tf_op jit(solution)/shard_map/all_to_all | solution.py:34
  160.0 1.9 copy.70
  161.9 1.9 reshape.249
  163.7 5.8 %all-to-all-start.5 = ((bf16[64,2,1536]{2,1,0:T(2,128)(2,1)}), bf16[64,2,1536]{2,1,0:T(2,128)(2,1)S(1)}, u32[]{:S(2)}, u32[]{:S(2)}) async-start(bf16[64,2,1536]{2,1,0:T(2,128)(2,1)} %reshape.249), calls=%async_computation.5 | async-start | bytes 786432 | tf_op jit(solution)/shard_map/all_to_all | solution.py:68
  169.7 13.0 %all-to-all-done.5 = bf16[64,2,1536]{2,1,0:T(2,128)(2,1)S(1)} async-done(((bf16[64,2,1536]{2,1,0:T(2,128)(2,1)}), bf16[64,2,1536]{2,1,0:T(2,128)(2,1)S(1)}, u32[]{:S(2)}, u32[]{:S(2)}) %all-to-all-start.5) | async-done | bytes 393248 | tf_op jit(solution)/shard_map/all_to_all | solution.py:68
  183.5 2.9 %copy.82 = bf16[32,2,64,48]{3,0,1,2:T(8,128)(2,1)} copy(bf16[32,2,64,48]{0,1,3,2:T(2,128)(2,1)S(1)} %bitcast.123) | data formatting | bytes 786432 | tf_op jit(solution)/shard_map/all_to_all | solution.py:68
  186.4 3.3 %add_convert_fusion = bf16[32,48,512]{2,1,0:T(8,128)(2,1)} fusion(bf16[32,48,512]{2,1,0:T(8,128)(2,1)S(1)} %copy-done.1, pred[32,512]{1,0:T(8,128)(4,1)S(1)} %iota_compare_fusion.1, bf16[32,128,48]{2,0,1:T(8,128)(2,1)} %bitcast.127, bf16[512,128]{0,1:T(8,128)(2,1)} %copy-done.2), kind=kOutput, calls=%fused_computation.7 | convolution fusion | flops 204472320 | bytes 3686400 | tf_op jit(solution)/shard_map/jda,dw->jaw/dot_general | solution.py:130
  (34 shorter events, 7.8 us)
Async XLA Ops:
  6.8 26.7 %all-to-all-start = ((bf16[64,2,1536]{2,1,0:T(2,128)(2,1)}), bf16[64,2,1536]{2,1,0:T(2,128)(2,1)S(1)}, u32[]{:S(2)}, u32[]{:S(2)}) async-start(bf16[64,2,1536]{2,1,0:T(2,128)(2,1)} %reshape.247), calls=%async_computation | async-start | bytes 786432 | tf_op jit(solution)/shard_map/all_to_all | solution.py:64
  38.5 27.6 %all-to-all-start.1 = ((bf16[4,32,2,3072]{3,1,2,0:T(8,128)(2,1)}), bf16[4,32,2,3072]{3,1,2,0:T(8,128)(2,1)S(1)}, u32[]{:S(2)}, u32[]{:S(2)}) async-start(bf16[4,32,2,3072]{3,1,2,0:T(8,128)(2,1)} %broadcast_in_dim.36), calls=%async_computation.1 | async-start | bytes 3145728 | tf_op jit(solution)/shard_map/all_to_all | solution.py:13
  66.2 5.1 %copy-start = (bf16[1,2,768,3072]{3,2,1,0:T(8,128)(2,1)S(1)}, bf16[1,2,768,3072]{3,2,1,0:T(8,128)(2,1)}, u32[]{:S(2)}) copy-start(bf16[1,2,768,3072]{3,2,1,0:T(8,128)(2,1)} %broadcast_multiply_fusion) | copy-start | bytes 28311556
  75.5 6.8 %copy-start.3 = (s32[128]{0:T(128)S(1)}, s32[128]{0:T(128)}, u32[]{:S(2)}) copy-start(s32[128]{0:T(128)} %param.6) | copy-start | bytes 1540
  76.7 18.6 %all-to-all-start.2 = ((bf16[128,2,768]{0,1,2:T(2,128)(2,1)}), bf16[128,2,768]{0,1,2:T(2,128)(2,1)S(1)}, u32[]{:S(2)}, u32[]{:S(2)}) async-start(bf16[128,2,768]{0,1,2:T(2,128)(2,1)} %copy.59), calls=%async_computation.2 | async-start | bytes 786432 | tf_op jit(solution)/shard_map/all_to_all | solution.py:68
  82.4 37.4 %copy-start.2 = (bf16[512,128]{0,1:T(8,128)(2,1)}, bf16[512,128]{0,1:T(8,128)(2,1)S(1)}, u32[]{:S(2)}) copy-start(bf16[512,128]{0,1:T(8,128)(2,1)S(1)} %convert_element_type.70) | copy-start | bytes 393220
  163.7 22.6 %copy-start.1 = (bf16[32,48,512]{2,1,0:T(8,128)(2,1)S(1)}, bf16[32,48,512]{2,1,0:T(8,128)(2,1)}, u32[]{:S(2)}) copy-start(bf16[32,48,512]{2,1,0:T(8,128)(2,1)} %param.4) | copy-start | bytes 4718596
  163.7 18.9 %all-to-all-start.5 = ((bf16[64,2,1536]{2,1,0:T(2,128)(2,1)}), bf16[64,2,1536]{2,1,0:T(2,128)(2,1)S(1)}, u32[]{:S(2)}, u32[]{:S(2)}) async-start(bf16[64,2,1536]{2,1,0:T(2,128)(2,1)} %reshape.249), calls=%async_computation.5 | async-start | bytes 786432 | tf_op jit(solution)/shard_map/all_to_all | solution.py:68
where the time goes:
time: 191 us; the launch traced here: 190 us
  blocking collectives  48.4 us (25%)
  waiting for transfers between devices  44.1 us (23%)
  starting transfers between devices  31.8 us (17%)
  local copies, waits for them, and re-layouts  27.4 us (14%)
  matrix products  26.9 us (14%)
  other arithmetic  10.7 us (6%)
    all_to_all x1, blocking collectives, sent_and_summed(): lax.all_to_all(split_up(array, dim, devices), axis, 0, 0, tiled=True)  26.5 us
    all_to_all x2, waiting for transfers between devices, to_time(): lax.all_to_all(values, 'wide', split_axis=2, concat_axis=1, tiled=True)  25.8 us
    all_to_all x1, blocking collectives, to_freq(): lax.all_to_all(values, 'wide', split_axis=1, concat_axis=2, tiled=True)  21.9 us
    all_to_all x1, starting transfers between devices, to_freq(): lax.all_to_all(values, 'wide', split_axis=1, concat_axis=2, tiled=True)  13.7 us
    unnamed x13, local copies, waits for them, and re-layouts  12.8 us
    all_to_all x1, waiting for transfers between devices, from_everyone(): return lax.all_to_all(copies, axis, split_axis=0, concat_axis=0, tiled=True)  11.9 us
    all_to_all x2, starting transfers between devices, to_time(): lax.all_to_all(values, 'wide', split_axis=2, concat_axis=1, tiled=True)  11.1 us
    mul x1, other arithmetic, masked_panel(): kernel.reshape(freq_dev, 2, row_blocks, TILE, col_blocks, TILE)  8.67 us
  transfers between devices with their start and end apart: 4, of which 4 were waited for; matrix products, arithmetic and copies ran while one was open for 8% of the time, Pallas kernels for 0%

commit v1 on v0

v1 whole, which is shorter than its diff:
```python
import functools

import jax
import jax.numpy as jnp
import numpy as np
from jax import lax
from jax.experimental import pallas as pl
from jax.experimental.pallas import tpu as pltpu
from jax.sharding import PartitionSpec as P

TILE = 256
NG = 4
GW = 16
CH = 24
F32 = jnp.float32
BF16 = jnp.bfloat16


def make_tables(bins, length):
    k = np.arange(1, bins + 1)
    t = np.arange(length)
    phase = (t[:, None] * k[None, :] % length).astype(np.float32) * np.float32(
        2.0 * np.pi / length
    )
    table = np.concatenate([np.cos(phase), -np.sin(phase)], axis=1)
    fwd = jnp.asarray(table, F32).astype(BF16)
    invt = jnp.asarray(table * (2.0 / length), F32).astype(BF16)
    return fwd, fwd.T, invt.T, invt


def wide_peer(me, d):
    x, loc = lax.div(me, GW), lax.rem(me, GW)
    i, n = lax.div(d, GW), lax.rem(d, GW)
    z, y = lax.div(loc, 2), lax.rem(loc, 2)
    tx = lax.rem(x + i, NG)
    tz = lax.rem(z + lax.div(n, 2), 8)
    ty = lax.rem(y + lax.rem(n, 2), 2)
    return tx * GW + tz * 2 + ty


def send(src, dst, ssem, rsem, wide, half):
    pltpu.make_async_remote_copy(
        src_ref=src,
        dst_ref=dst,
        send_sem=ssem,
        recv_sem=rsem,
        device_id={"wide": wide, "half": half},
        device_id_type=pl.DeviceIdType.MESH,
    ).start()


def await_bytes(ref, sem):
    pltpu.make_async_copy(ref, ref, sem).wait()


def focus_kernel(
    focus_hbm, kern_hbm, mask_ref, onset_ref, fwd_ref, fwdt_ref, invt_ref,
    out_ref,
    xv, mv, big, tr, v1, r1, fv, s2, r2, s3, h3, ht, pv, rs, qv, zs, zv, s4, r4,
    sem_x, sem_m, snd, rcv1, rel, rcv2, rcv3, rcvq, rcvz, rcv4, loc_sem,
):
    me = lax.axis_index("wide")
    hf = lax.axis_index("half")
    x = lax.div(me, GW)
    yh, q = lax.div(hf, 2), lax.rem(hf, 2)
    partner = yh * 2 + (1 - q)
    ypeer = (1 - yh) * 2 + q
    diag = (1 - yh) * 2 + (1 - q)
    copy_x = pltpu.make_async_copy(focus_hbm, xv, sem_x)
    copy_x.start()
    copy_m = pltpu.make_async_copy(kern_hbm, mv, sem_m)
    copy_m.start()
    barrier = pltpu.get_barrier_semaphore()

    @pl.loop(1, NG * GW)
    def _(d):
        pl.semaphore_signal(
            barrier,
            inc=1,
            device_id={"wide": wide_peer(me, d), "half": hf},
            device_id_type=pl.DeviceIdType.MESH,
        )

    for other in (partner, ypeer):
        pl.semaphore_signal(
            barrier,
            inc=1,
            device_id={"wide": me, "half": other},
            device_id_type=pl.DeviceIdType.MESH,
        )

    lane = lax.broadcasted_iota(jnp.int32, (1, 128), 1)
    low64 = lane < 64
    low32 = lax.rem(lane, 64) < 32

    copy_x.wait()
    for b in range(4):
        rows = pl.ds(b * 384, 384)
        big[rows, :] = jnp.dot(xv[rows, :], fwd_ref[...], preferred_element_type=F32)

    @pl.loop(0, 12)
    def _(jp):
        j = 2 * jp
        a = [
            [big[pl.ds(s * CH + j + jj, 32, stride=48), :] for jj in range(2)]
            for s in range(2)
        ]
        first = [jnp.where(low64, a[s][0], pltpu.roll(a[s][1], 64, 1)) for s in range(2)]
        second = [jnp.where(low64, pltpu.roll(a[s][0], 64, 1), a[s][1]) for s in range(2)]
        t = jnp.concatenate(first + second, axis=0).T
        tr[pl.ds(j, 64, stride=CH), :] = t[:64]
        tr[pl.ds(j + 1, 64, stride=CH), :] = t[64:]

    for b in range(4):
        v1[pl.ds(b * 16, 16)] = tr[pl.ds(b * 384, 384), :].astype(BF16).reshape(16, CH, 128)

    pl.semaphore_wait(barrier, NG * GW - 1 + 2)

    pltpu.make_async_copy(v1.at[me], r1.at[hf, me], rcv1.at[x]).start()

    @pl.loop(1, NG * GW)
    def _(d):
        peer = wide_peer(me, d)
        send(v1.at[peer], r1.at[hf, me], snd.at[0], rcv1.at[x], peer, hf)

    copy_m.wait()

    @pl.loop(0, 36)
    def _(n):
        a, b = lax.div(n, 12), lax.rem(n, 12)
        keep = mask_ref[hf * 3 + a, b].astype(F32)
        keep = jnp.full((TILE, TILE), keep, F32).astype(BF16)
        rows = pl.ds(pl.multiple_of(a * TILE, TILE), TILE)
        cols = pl.ds(pl.multiple_of(b * TILE, TILE), TILE)
        for c in range(2):
            mv[c, rows, cols] = mv[c, rows, cols] * keep

    def group(i):
        return lax.rem(x - i + NG, NG)

    def slab(g):
        return pl.ds(g * GW, GW)

    @pl.loop(0, NG)
    def _(i):
        g = group(i)
        own = r1.at[hf, slab(g)]
        await_bytes(own, rcv1.at[g])
        send(own, own, snd.at[1], rel.at[0, g], me, ypeer)
        send(own, own, snd.at[1], rel.at[1, g], me, partner)

    @pl.loop(0, NG)
    def _(i):
        g = group(i)
        theirs = r1.at[ypeer, slab(g)]
        await_bytes(theirs, rel.at[0, g])
        send(theirs, theirs, snd.at[1], rel.at[2, g], me, partner)

    @pl.loop(0, NG)
    def _(i):
        g = group(i)
        await_bytes(r1.at[partner, slab(g)], rel.at[1, g])
        await_bytes(r1.at[diag, slab(g)], rel.at[2, g])

        @pl.loop(0, GW)
        def _(n):
            w = g * GW + n
            rows = pl.ds(pl.multiple_of(w * 48, 48), 48)
            for t in range(2):
                b0 = r1[2 * t, w].astype(F32)
                b1 = r1[2 * t + 1, w].astype(F32)
                o0 = jnp.where(low32, b0, pltpu.roll(b1, 32, 1))
                o1 = jnp.where(low32, pltpu.roll(b0, 96, 1), b1)
                fv[rows, t * 128 : (t + 1) * 128] = jnp.concatenate([o0, o1], axis=0).astype(BF16)

    sign = jnp.where(low64, -1.0, 1.0).astype(F32)

    @pl.loop(0, NG)
    def _(i):
        b = lax.rem(x + i, NG)
        rows = pl.ds(pl.multiple_of(b * 192, 192), 192)
        lhs = jnp.concatenate([mv[0, rows, :], mv[1, rows, :]], axis=0)
        acc = jnp.dot(lhs, fv[...], preferred_element_type=F32)
        for t in range(2):
            re = acc[:192, t * 128 : (t + 1) * 128]
            im = acc[192:, t * 128 : (t + 1) * 128]
            wv = re + sign * pltpu.roll(im, 64, 1)
            s2[t, pl.ds(b * 8, 8)] = wv.astype(BF16).reshape(8, CH, 128)

        @pl.loop(0, GW)
        def _(n):
            peer = wide_peer(me, i * GW + n)
            src = s2.at[lax.rem(peer, 2), lax.div(peer, 2)]

            @pl.when(i + n > 0)
            def _():
                send(src, r2.at[me], snd.at[2], rcv2, peer, hf)

            @pl.when(i + n == 0)
            def _():
                pltpu.make_async_copy(src, r2.at[me], rcv2).start()

    await_bytes(r2, rcv2)

    for b in range(4):
        big[pl.ds(b * 384, 384), :] = r2[pl.ds(b * 16, 16)].astype(F32).reshape(384, 128)
    mine = onset_ref[pl.ds(lax.rem(me, 2), 1), :]
    mute = lax.broadcasted_iota(jnp.int32, (512, 128), 0) < mine
    mute = jnp.concatenate([mute, mute], axis=1)

    @pl.loop(0, 6)
    def _(rq):
        cols = []
        for u in range(2):
            r = rq * 4 + u * 2
            a0 = big[pl.ds(r, 64, stride=CH), :]
            a1 = big[pl.ds(r + 1, 64, stride=CH), :]
            top = jnp.where(low64, a0, pltpu.roll(a1, 64, 1))
            bot = jnp.where(low64, pltpu.roll(a0, 64, 1), a1)
            cols.append(jnp.concatenate([top, bot], axis=0))
        spec = jnp.concatenate(cols, axis=1).astype(BF16)
        trace = jnp.dot(invt_ref[...], spec, preferred_element_type=F32)
        muted = jnp.where(mute, trace, 0.0).astype(BF16)
        back = jnp.dot(fwdt_ref[...], muted, preferred_element_type=F32)
        for u in range(2):
            r = rq * 4 + u * 2
            top = back[:64, u * 128 : (u + 1) * 128]
            bot = back[64:, u * 128 : (u + 1) * 128]
            tr[pl.ds(r, 64, stride=CH), :] = jnp.where(low64, top, pltpu.roll(bot, 64, 1))
            tr[pl.ds(r + 1, 64, stride=CH), :] = jnp.where(low64, pltpu.roll(top, 64, 1), bot)

    for b in range(4):
        s3[pl.ds(b * 16, 16)] = tr[pl.ds(b * 384, 384), :].astype(BF16).reshape(16, CH, 128)
    slot = (lax.rem(me, 2), lax.div(me, 2))
    pltpu.make_async_copy(s3.at[me], h3.at[slot], rcv3).start()

    @pl.loop(1, NG * GW)
    def _(d):
        peer = wide_peer(me, d)
        send(s3.at[peer], h3.at[slot], snd.at[3], rcv3, peer, hf)

    await_bytes(h3, rcv3)

    for t in range(2):
        for b in range(2):
            piece = h3[t, pl.ds(b * 16, 16)].astype(F32).reshape(384, 128)
            for u in range(3):
                ht[t * 128 : (t + 1) * 128, b * 384 + u * 128 : b * 384 + (u + 1) * 128] = (
                    piece[u * 128 : (u + 1) * 128].T.astype(BF16)
                )

    @pl.loop(0, NG + 2)
    def _(i):
        @pl.when(i < NG)
        def _():
            g = lax.rem(x + i, NG)
            for b in range(3):
                cols = pl.ds(pl.multiple_of(g * 768 + b * TILE, TILE), TILE)
                pa = jnp.dot(ht[...], mv[0, :, cols], preferred_element_type=F32)
                pb = jnp.dot(ht[...], mv[1, :, cols], preferred_element_type=F32)
                pc = jnp.concatenate(
                    [
                        pa[0:64] + pb[64:128],
                        pa[64:128] - pb[0:64],
                        pa[128:192] + pb[192:256],
                        pa[192:256] - pb[128:192],
                    ],
                    axis=0,
                )
                pv[b * TILE : (b + 1) * TILE, :] = pc.T

            @pl.loop(0, GW)
            def _(n):
                w = g * GW + n
                for t in range(2):
                    base = pl.multiple_of(n * 48, 8)
                    i0 = pv[pl.ds(base, CH), t * 128 : (t + 1) * 128]
                    i1 = pv[pl.ds(pl.multiple_of(base + CH, 8), CH), t * 128 : (t + 1) * 128]
                    rs[2 * t, w] = jnp.where(low32, i0, pltpu.roll(i1, 32, 1)).astype(BF16)
                    rs[2 * t + 1, w] = jnp.where(low32, pltpu.roll(i0, 96, 1), i1).astype(BF16)

            for t in range(2):
                send(
                    rs.at[2 * t + (1 - q), slab(g)], qv.at[t, slab(g)],
                    snd.at[4], rcvq.at[t, g], me, partner,
                )

        @pl.when(jnp.logical_and(i >= 1, i <= NG))
        def _():
            g = lax.rem(x + i - 1, NG)
            t = 1 - yh
            await_bytes(qv.at[t, slab(g)], rcvq.at[t, g])
            total = rs[2 * t + q, slab(g)].astype(F32) + qv[t, slab(g)].astype(F32)
            zs[slab(g)] = total.astype(BF16)
            send(zs.at[slab(g)], zv.at[slab(g)], snd.at[5], rcvz.at[g], me, ypeer)

        @pl.when(i >= 2)
        def _():
            g = lax.rem(x + i - 2, NG)
            await_bytes(qv.at[yh, slab(g)], rcvq.at[yh, g])
            await_bytes(zv.at[slab(g)], rcvz.at[g])
            total = rs[hf, slab(g)].astype(F32) + qv[yh, slab(g)].astype(F32)
            s4[slab(g)] = (total + zv[slab(g)].astype(F32)).astype(BF16)

            @pl.loop(0, GW)
            def _(n):
                peer = wide_peer(me, (i - 2) * GW + n)

                @pl.when(i - 2 + n > 0)
                def _():
                    send(s4.at[peer], r4.at[me], snd.at[6], rcv4, peer, hf)

                @pl.when(i - 2 + n == 0)
                def _():
                    pltpu.make_async_copy(s4.at[peer], r4.at[me], rcv4).start()

    await_bytes(r4, rcv4)

    for b in range(4):
        big[pl.ds(b * 384, 384), :] = r4[pl.ds(b * 16, 16)].astype(F32).reshape(384, 128)

    @pl.loop(0, 12)
    def _(jp):
        j = 2 * jp
        a0 = big[pl.ds(j, 64, stride=CH), :]
        a1 = big[pl.ds(j + 1, 64, stride=CH), :]
        t = jnp.concatenate([a0, a1], axis=0).T
        l0 = jnp.where(low64, t[:64], pltpu.roll(t[64:], 64, 1))
        l1 = jnp.where(low64, pltpu.roll(t[:64], 64, 1), t[64:])
        for s in range(2):
            tr[pl.ds(s * CH + j, 32, stride=48), :] = l0[s * 32 : (s + 1) * 32]
            tr[pl.ds(s * CH + j + 1, 32, stride=48), :] = l1[s * 32 : (s + 1) * 32]

    for b in range(4):
        rows = pl.ds(b * 384, 384)
        out_ref[rows, :] = tr[rows, :].astype(BF16)

    n63 = pl.ds(0, NG * GW - 1)
    await_bytes(v1.at[n63], snd.at[0])
    await_bytes(r1.at[pl.ds(0, 3)], snd.at[1])
    await_bytes(r2.at[n63], snd.at[2])
    await_bytes(s3.at[n63], snd.at[3])
    await_bytes(rs.at[pl.ds(0, 2)], snd.at[4])
    await_bytes(zs, snd.at[5])
    await_bytes(s4.at[n63], snd.at[6])


def spectra_loop(focus, kern, tile_mask, onset2, fwd, fwdt, invt):
    dma = pltpu.SemaphoreType.DMA
    vmem = pl.BlockSpec(memory_space=pltpu.VMEM)
    hbm = pl.BlockSpec(memory_space=pl.ANY)
    smem = pl.BlockSpec(memory_space=pltpu.SMEM)
    chunk = (CH, 128)
    return pl.pallas_call(
        focus_kernel,
        out_shape=jax.ShapeDtypeStruct((1536, 128), BF16),
        in_specs=[hbm, hbm, smem, vmem, vmem, vmem, vmem],
        out_specs=vmem,
        scratch_shapes=[
            pltpu.VMEM((1536, 512), BF16),
            pltpu.VMEM((2, 768, 3072), BF16),
            pltpu.VMEM((1536, 128), F32),
            pltpu.VMEM((1536, 128), F32),
            pltpu.VMEM((64, *chunk), BF16),
            pltpu.VMEM((4, 64, *chunk), BF16),
            pltpu.VMEM((3072, 256), BF16),
            pltpu.VMEM((2, 32, *chunk), BF16),
            pltpu.VMEM((64, *chunk), BF16),
            pltpu.VMEM((64, *chunk), BF16),
            pltpu.VMEM((2, 32, *chunk), BF16),
            pltpu.VMEM((256, 768), BF16),
            pltpu.VMEM((768, 256), F32),
            pltpu.VMEM((4, 64, *chunk), BF16),
            pltpu.VMEM((2, 64, *chunk), BF16),
            pltpu.VMEM((64, *chunk), BF16),
            pltpu.VMEM((64, *chunk), BF16),
            pltpu.VMEM((64, *chunk), BF16),
            pltpu.VMEM((64, *chunk), BF16),
            dma, dma, dma((7,)), dma((NG,)), dma((3, NG)), dma, dma,
            dma((2, NG)), dma((NG,)), dma, dma,
        ],
        compiler_params=pltpu.CompilerParams(
            collective_id=0, has_side_effects=True, vmem_limit_bytes=60 * 1024 * 1024
        ),
        name="focus_update",
    )(focus, kern, tile_mask, onset2, fwd, fwdt, invt)


def finish_kernel(points, onset_ref, spec_ref, focus_ref, inv_ref, out_ref):
    i = pl.program_id(0)
    upd = jnp.dot(spec_ref[...], inv_ref[...], preferred_element_type=F32)
    time = lax.broadcasted_iota(jnp.int32, (48, 512), 1)
    for n in range(points):
        kept = jnp.where(time < onset_ref[i * points + n], upd[n * 48 : (n + 1) * 48], 0.0)
        out_ref[n] = (focus_ref[n].astype(F32) + kept).astype(BF16)


def finish(onset, spec, focus, inv):
    points = 8
    return pl.pallas_call(
        functools.partial(finish_kernel, points),
        out_shape=jax.ShapeDtypeStruct(focus.shape, BF16),
        grid=(32 // points,),
        in_specs=[
            pl.BlockSpec(memory_space=pltpu.SMEM),
            pl.BlockSpec((points * 48, 128), lambda i: (i, 0)),
            pl.BlockSpec((points, 48, 512), lambda i: (i, 0, 0)),
            pl.BlockSpec((128, 512), lambda i: (0, 0)),
        ],
        out_specs=pl.BlockSpec((points, 48, 512), lambda i: (i, 0, 0)),
        name="finish",
    )(onset, spec, focus, inv)


def shards(focus, kernel, onset, tile_mask):
    own_points, local_receivers, length = focus.shape
    fwd, fwdt, inv, invt = make_tables(64, length)
    halves = onset.reshape(2, 64)
    spec = spectra_loop(
        focus.reshape(own_points * local_receivers, length),
        kernel[0],
        tile_mask,
        jnp.concatenate([halves, halves], axis=1),
        fwd, fwdt, invt,
    )
    mine = lax.dynamic_slice_in_dim(onset, lax.axis_index("half") * own_points, own_points, 0)
    return finish(mine, spec, focus, inv)


def solution(mesh):
    in_specs = (P("half", "wide", None), P("wide", None, "half", None), P(), P())
    out_specs = P("half", "wide", None)
    return jax.shard_map(shards, mesh=mesh, in_specs=in_specs, out_specs=out_specs, check_vma=False)
```

time: 191 us -> 101 us (0.53)
  Pallas kernels: 0 us -> 97.9 us
  blocking collectives: 48.4 us -> 0 us
  waiting for transfers between devices: 44.1 us -> 0 us
  starting transfers between devices: 31.8 us -> 0 us
  matrix products: 26.9 us -> 0 us
  local copies, waits for them, and re-layouts: 27.4 us -> 2.04 us
  other arithmetic: 10.7 us -> 0.64 us
    pallas_call x0 -> x2, Pallas kernels: none -> 97.9 us  [the longest x1 93.7 us: spectra_loop(): pl.pallas_call(focus_kernel, out_shape=jax.ShapeDtypeStruct((1536, 128),...]
    all_to_all x2 -> x0, blocking collectives: 48.4 us -> none  [the longest x1 26.5 us: sent_and_summed(): lax.all_to_all(split_up(array, dim, devices), axis, 0, 0, tiled=True)]
    all_to_all x4 -> x0, waiting for transfers between devices: 44.1 us -> none  [the longest x2 25.8 us: to_time(): lax.all_to_all(values, 'wide', split_axis=2, concat_axis=1, tiled=True)]
    all_to_all x4 -> x0, starting transfers between devices: 31.8 us -> none  [the longest x1 13.7 us: to_freq(): lax.all_to_all(values, 'wide', split_axis=1, concat_axis=2, tiled=True)]
    dot_general x11 -> x0, matrix products: 26.9 us -> none  [the longest x1 3.87 us: forward_waves(): jnp.einsum('pfs,frs->pfr', split[:, :, 0], kernel_real, preferred_element...]
    unnamed x13 -> x0, local copies, waits for them, and re-layouts: 12.8 us -> none
    mul x1 -> x0, other arithmetic: 8.67 us -> none  [masked_panel(): kernel.reshape(freq_dev, 2, row_blocks, TILE, col_blocks, TILE)]
    all_to_all x6 -> x0, local copies, waits for them, and re-layouts: 6.32 us -> none  [the longest x2 3.21 us: to_time(): lax.all_to_all(values, 'wide', split_axis=2, concat_axis=1, tiled=True)]
  transfers between devices with their start and end apart: 4 -> 0, of which waited for: 4 -> 0; matrix products, arithmetic and copies ran while one was open for 8% -> 0% of each run, Pallas kernels for 0% -> 0%
where the time goes in v1:
time: 101 us
  Pallas kernels  97.9 us (97%)
  local copies, waits for them, and re-layouts  2.04 us (2%)
    pallas_call x1, Pallas kernels, spectra_loop(): pl.pallas_call(focus_kernel, out_shape=jax.ShapeDtypeStruct((1536, 128),...  93.7 us
    pallas_call x1, Pallas kernels, finish(): pl.pallas_call(functools.partial(finish_kernel, points), out_shape=jax.Sh...  4.18 us

profile of v1, /device:TPU:1, one launch (start us, length us, event | category | flops | bytes accessed | tf_op | source)
XLA Modules:
  0.0 100.6 jit_solution(10579549681459527534)
XLA Ops:
  0.0 1.3 %dynamic_slice.3.onset_ref = s32[32]{0:T(128)} dynamic-slice(s32[128]{0:T(128)} %param.8, s32[]{:T(128)S(6)} %select_n.3), dynamic_slice_sizes={32} | dynamic-slice | bytes 260 | tf_op jit(solution)/shard_map/dynamic_slice | solution.py:426
  1.3 0.7 reshape.7
  2.0 0.6 pad_add_fusion.onset_ref
  2.7 93.7 %focus_update.1.spec_ref = bf16[1536,128]{1,0:T(8,128)(2,1)} custom-call(bf16[1536,512]{1,0:T(8,128)(2,1)} %bitcast.3, bf16[2,768,3072]{2,1,0:T(8,128)(2,1)} %bitcast.2, s32[12,12]{1,0:T(8,128)} %mask_ref.1, s32[2,128]{1,0:T(2,128)} %pad_add_fusion.onset_ref, bf16[512,128]{1,0:T(8,128)(2,1)} %constant.18.fwd_ref, bf16[128,512]{1,0:T(8,128)(2,1)} %constant.19.fwdt_ref, ...), custom_call_target="tpu_custom_call" | custom-call | tf_op jit(solution)/shard_map/focus_update/pallas_call | solution.py:354
  96.4 4.2 %finish.1 = bf16[32,48,512]{2,1,0:T(8,128)(2,1)} custom-call(s32[32]{0:T(128)} %dynamic_slice.3.onset_ref, bf16[1536,128]{1,0:T(8,128)(2,1)} %focus_update.1.spec_ref, bf16[32,48,512]{2,1,0:T(8,128)(2,1)} %focus_ref.1, bf16[128,512]{1,0:T(8,128)(2,1)} %constant.21.inv_ref), custom_call_target="tpu_custom_call" | custom-call | tf_op jit(solution)/shard_map/finish/pallas_call | solution.py:400

commit v2 on v1

--- a/solution.py
+++ b/solution.py
@@ -56,8 +56,8 @@
 def focus_kernel(
     focus_hbm, kern_hbm, mask_ref, onset_ref, fwd_ref, fwdt_ref, invt_ref,
     out_ref,
-    xv, mv, big, tr, v1, r1, fv, s2, r2, s3, h3, ht, pv, rs, qv, zs, zv, s4, r4,
-    sem_x, sem_m, snd, rcv1, rel, rcv2, rcv3, rcvq, rcvz, rcv4, loc_sem,
+    xv, mv, big, tr, v1, b1, r1, fv, acc, s2, r2, s3, h3, ht, pv, rs, qv, zs, zr, s4, r4,
+    sem_x, sem_m, snd, rcva, rcvb, rel, chip, rcv2, rcv3, rcvq, rcvz, rcv4,
 ):
     me = lax.axis_index("wide")
     hf = lax.axis_index("half")
@@ -65,7 +65,8 @@
     yh, q = lax.div(hf, 2), lax.rem(hf, 2)
     partner = yh * 2 + (1 - q)
     ypeer = (1 - yh) * 2 + q
-    diag = (1 - yh) * 2 + (1 - q)
+    z, yl = lax.div(lax.rem(me, GW), 2), lax.rem(me, 2)
+    beside = x * GW + 2 * z + (1 - yl)
     copy_x = pltpu.make_async_copy(focus_hbm, xv, sem_x)
     copy_x.start()
     copy_m = pltpu.make_async_copy(kern_hbm, mv, sem_m)
@@ -81,11 +82,11 @@
             device_id_type=pl.DeviceIdType.MESH,
         )
 
-    for other in (partner, ypeer):
+    for w, other in ((me, partner), (me, ypeer), (beside, ypeer)):
         pl.semaphore_signal(
             barrier,
             inc=1,
-            device_id={"wide": me, "half": other},
+            device_id={"wide": w, "half": other},
             device_id_type=pl.DeviceIdType.MESH,
         )
 
@@ -114,14 +115,21 @@
     for b in range(4):
         v1[pl.ds(b * 16, 16)] = tr[pl.ds(b * 384, 384), :].astype(BF16).reshape(16, CH, 128)
 
-    pl.semaphore_wait(barrier, NG * GW - 1 + 2)
-
-    pltpu.make_async_copy(v1.at[me], r1.at[hf, me], rcv1.at[x]).start()
-
-    @pl.loop(1, NG * GW)
+    pl.semaphore_wait(barrier, NG * GW - 1 + 3)
+
+    here = x * 8 + z
+    own_k = here * 2
+    pltpu.make_async_copy(v1.at[me], r1.at[hf, x, yl, z], rcva.at[x]).start()
+    pltpu.make_async_copy(v1.at[own_k + 1 - yl], b1.at[here], rcvb.at[x]).start()
+
+    @pl.loop(1, 32)
     def _(d):
-        peer = wide_peer(me, d)
-        send(v1.at[peer], r1.at[hf, me], snd.at[0], rcv1.at[x], peer, hf)
+        tx = lax.rem(x + lax.div(d, 8), NG)
+        tz = lax.rem(z + lax.rem(d, 8), 8)
+        k = tx * GW + tz * 2
+        peer = k + yl
+        send(v1.at[peer], r1.at[hf, x, yl, z], snd.at[0], rcva.at[x], peer, hf)
+        send(v1.at[k + 1 - yl], b1.at[here], snd.at[0], rcvb.at[x], peer, hf)
 
     copy_m.wait()
 
@@ -135,55 +143,72 @@
         for c in range(2):
             mv[c, rows, cols] = mv[c, rows, cols] * keep
 
-    def group(i):
-        return lax.rem(x - i + NG, NG)
+    acc[...] = jnp.zeros_like(acc)
+    sign = jnp.where(low64, -1.0, 1.0).astype(F32)
 
     def slab(g):
-        return pl.ds(g * GW, GW)
-
-    @pl.loop(0, NG)
+        return pl.ds(g * 8, 8)
+
+    def product(g, b):
+        rows = pl.ds(pl.multiple_of(b * 192, 192), 192)
+        cols = pl.ds(pl.multiple_of(g * 768, 768), 768)
+        lhs = jnp.concatenate([mv[0, rows, cols], mv[1, rows, cols]], axis=0)
+        return jnp.dot(lhs, fv[...], preferred_element_type=F32)
+
+    @pl.loop(0, NG + 2)
     def _(i):
-        g = group(i)
-        own = r1.at[hf, slab(g)]
-        await_bytes(own, rcv1.at[g])
-        send(own, own, snd.at[1], rel.at[0, g], me, ypeer)
-        send(own, own, snd.at[1], rel.at[1, g], me, partner)
-
-    @pl.loop(0, NG)
-    def _(i):
-        g = group(i)
-        theirs = r1.at[ypeer, slab(g)]
-        await_bytes(theirs, rel.at[0, g])
-        send(theirs, theirs, snd.at[1], rel.at[2, g], me, partner)
-
-    @pl.loop(0, NG)
-    def _(i):
-        g = group(i)
-        await_bytes(r1.at[partner, slab(g)], rel.at[1, g])
-        await_bytes(r1.at[diag, slab(g)], rel.at[2, g])
-
-        @pl.loop(0, GW)
-        def _(n):
-            w = g * GW + n
-            rows = pl.ds(pl.multiple_of(w * 48, 48), 48)
-            for t in range(2):
-                b0 = r1[2 * t, w].astype(F32)
-                b1 = r1[2 * t + 1, w].astype(F32)
-                o0 = jnp.where(low32, b0, pltpu.roll(b1, 32, 1))
-                o1 = jnp.where(low32, pltpu.roll(b0, 96, 1), b1)
-                fv[rows, t * 128 : (t + 1) * 128] = jnp.concatenate([o0, o1], axis=0).astype(BF16)
-
-    sign = jnp.where(low64, -1.0, 1.0).astype(F32)
+        @pl.when(i < NG)
+        def _():
+            g = lax.rem(x - i + NG, NG)
+            own = r1.at[hf, g, yl]
+            await_bytes(own, rcva.at[g])
+            send(own, own, snd.at[1], rel.at[0, g], me, ypeer)
+            send(own, own, snd.at[2], chip.at[0, g], me, partner)
+            await_bytes(b1.at[slab(g)], rcvb.at[g])
+            send(b1.at[slab(g)], own, snd.at[1], rel.at[1, g], beside, hf)
+            send(b1.at[slab(g)], own, snd.at[1], rel.at[2, g], beside, ypeer)
+
+        @pl.when(jnp.logical_and(i >= 1, i <= NG))
+        def _():
+            g = lax.rem(x - i + 1 + NG, NG)
+            for n, (h, y) in enumerate(((ypeer, yl), (hf, 1 - yl), (ypeer, 1 - yl))):
+                got = r1.at[h, g, y]
+                await_bytes(got, rel.at[n, g])
+                send(got, got, snd.at[2], chip.at[n + 1, g], me, partner)
+
+        @pl.when(i >= 2)
+        def _():
+            g = lax.rem(x - i + 2 + NG, NG)
+            diag = (1 - yh) * 2 + (1 - q)
+            for n, (h, y) in enumerate(
+                ((partner, yl), (diag, yl), (partner, 1 - yl), (diag, 1 - yl))
+            ):
+                await_bytes(r1.at[h, g, y], chip.at[n, g])
+
+            @pl.loop(0, GW)
+            def _(n):
+                at = (lax.rem(n, 2), lax.div(n, 2))
+                rows = pl.ds(pl.multiple_of(n * 48, 48), 48)
+                for t in range(2):
+                    b0 = r1[2 * t, g, at[0], at[1]].astype(F32)
+                    b1_ = r1[2 * t + 1, g, at[0], at[1]].astype(F32)
+                    o0 = jnp.where(low32, b0, pltpu.roll(b1_, 32, 1))
+                    o1 = jnp.where(low32, pltpu.roll(b0, 96, 1), b1_)
+                    fv[rows, t * 128 : (t + 1) * 128] = jnp.concatenate([o0, o1], axis=0).astype(BF16)
+
+            @pl.when(i < NG + 1)
+            def _():
+                @pl.loop(0, NG)
+                def _(b):
+                    acc[b] += product(g, b)
 
     @pl.loop(0, NG)
     def _(i):
         b = lax.rem(x + i, NG)
-        rows = pl.ds(pl.multiple_of(b * 192, 192), 192)
-        lhs = jnp.concatenate([mv[0, rows, :], mv[1, rows, :]], axis=0)
-        acc = jnp.dot(lhs, fv[...], preferred_element_type=F32)
+        full = acc[b] + product(lax.rem(x + 1, NG), b)
         for t in range(2):
-            re = acc[:192, t * 128 : (t + 1) * 128]
-            im = acc[192:, t * 128 : (t + 1) * 128]
+            re = full[:192, t * 128 : (t + 1) * 128]
+            im = full[192:, t * 128 : (t + 1) * 128]
             wv = re + sign * pltpu.roll(im, 64, 1)
             s2[t, pl.ds(b * 8, 8)] = wv.astype(BF16).reshape(8, CH, 128)
 
@@ -194,7 +219,7 @@
 
             @pl.when(i + n > 0)
             def _():
-                send(src, r2.at[me], snd.at[2], rcv2, peer, hf)
+                send(src, r2.at[me], snd.at[3], rcv2, peer, hf)
 
             @pl.when(i + n == 0)
             def _():
@@ -204,7 +229,11 @@
 
     for b in range(4):
         big[pl.ds(b * 384, 384), :] = r2[pl.ds(b * 16, 16)].astype(F32).reshape(384, 128)
-    mine = onset_ref[pl.ds(lax.rem(me, 2), 1), :]
+    points = jnp.broadcast_to(onset_ref[...], (8, 128))
+    other = pltpu.roll(points, 64, 1)
+    mine = jnp.where(
+        yl == 0, jnp.where(low64, points, other), jnp.where(low64, other, points)
+    )[0:1]
     mute = lax.broadcasted_iota(jnp.int32, (512, 128), 0) < mine
     mute = jnp.concatenate([mute, mute], axis=1)
 
@@ -237,7 +266,7 @@
     @pl.loop(1, NG * GW)
     def _(d):
         peer = wide_peer(me, d)
-        send(s3.at[peer], h3.at[slot], snd.at[3], rcv3, peer, hf)
+        send(s3.at[peer], h3.at[slot], snd.at[4], rcv3, peer, hf)
 
     await_bytes(h3, rcv3)
 
@@ -271,48 +300,51 @@
 
             @pl.loop(0, GW)
             def _(n):
-                w = g * GW + n
+                y, zz = lax.rem(n, 2), lax.div(n, 2)
                 for t in range(2):
                     base = pl.multiple_of(n * 48, 8)
                     i0 = pv[pl.ds(base, CH), t * 128 : (t + 1) * 128]
                     i1 = pv[pl.ds(pl.multiple_of(base + CH, 8), CH), t * 128 : (t + 1) * 128]
-                    rs[2 * t, w] = jnp.where(low32, i0, pltpu.roll(i1, 32, 1)).astype(BF16)
-                    rs[2 * t + 1, w] = jnp.where(low32, pltpu.roll(i0, 96, 1), i1).astype(BF16)
+                    rs[2 * t, g, y, zz] = jnp.where(low32, i0, pltpu.roll(i1, 32, 1)).astype(BF16)
+                    rs[2 * t + 1, g, y, zz] = jnp.where(low32, pltpu.roll(i0, 96, 1), i1).astype(BF16)
 
             for t in range(2):
-                send(
-                    rs.at[2 * t + (1 - q), slab(g)], qv.at[t, slab(g)],
-                    snd.at[4], rcvq.at[t, g], me, partner,
-                )
+                send(rs.at[2 * t + (1 - q), g], qv.at[t, g], snd.at[5], rcvq.at[t, g], me, partner)
 
         @pl.when(jnp.logical_and(i >= 1, i <= NG))
         def _():
             g = lax.rem(x + i - 1, NG)
-            t = 1 - yh
-            await_bytes(qv.at[t, slab(g)], rcvq.at[t, g])
-            total = rs[2 * t + q, slab(g)].astype(F32) + qv[t, slab(g)].astype(F32)
-            zs[slab(g)] = total.astype(BF16)
-            send(zs.at[slab(g)], zv.at[slab(g)], snd.at[5], rcvz.at[g], me, ypeer)
+            for t in range(2):
+                await_bytes(qv.at[t, g], rcvq.at[t, g])
+                total = rs[2 * t + q, g].astype(F32) + qv[t, g].astype(F32)
+                zs[t, g] = total.astype(BF16)
+            send(zs.at[1 - yh, g, 1 - yl], zr.at[2, g], snd.at[6], rcvz.at[2, g], beside, ypeer)
+            send(zs.at[yh, g, 1 - yl], zr.at[1, g], snd.at[6], rcvz.at[1, g], beside, hf)
+            send(zs.at[1 - yh, g, yl], zr.at[0, g], snd.at[6], rcvz.at[0, g], me, ypeer)
 
         @pl.when(i >= 2)
         def _():
             g = lax.rem(x + i - 2, NG)
-            await_bytes(qv.at[yh, slab(g)], rcvq.at[yh, g])
-            await_bytes(zv.at[slab(g)], rcvz.at[g])
-            total = rs[hf, slab(g)].astype(F32) + qv[yh, slab(g)].astype(F32)
-            s4[slab(g)] = (total + zv[slab(g)].astype(F32)).astype(BF16)
-
-            @pl.loop(0, GW)
+            for n in range(3):
+                await_bytes(zr.at[n, g], rcvz.at[n, g])
+            s4[yl, g] = (zs[yh, g, yl].astype(F32) + zr[0, g].astype(F32)).astype(BF16)
+            s4[1 - yl, g] = (zr[1, g].astype(F32) + zr[2, g].astype(F32)).astype(BF16)
+
+            @pl.loop(0, 8)
             def _(n):
-                peer = wide_peer(me, (i - 2) * GW + n)
+                tz = lax.rem(z + n, 8)
+                peer = g * GW + tz * 2 + yl
+                k = x * GW + z * 2
 
                 @pl.when(i - 2 + n > 0)
                 def _():
-                    send(s4.at[peer], r4.at[me], snd.at[6], rcv4, peer, hf)
+                    send(s4.at[0, g, tz], r4.at[k], snd.at[7], rcv4, peer, hf)
+                    send(s4.at[1, g, tz], r4.at[k + 1], snd.at[7], rcv4, peer, hf)
 
                 @pl.when(i - 2 + n == 0)
                 def _():
-                    pltpu.make_async_copy(s4.at[peer], r4.at[me], rcv4).start()
+                    pltpu.make_async_copy(s4.at[0, g, tz], r4.at[k], rcv4).start()
+                    pltpu.make_async_copy(s4.at[1, g, tz], r4.at[k + 1], rcv4).start()
 
     await_bytes(r4, rcv4)
 
@@ -336,13 +368,14 @@
         out_ref[rows, :] = tr[rows, :].astype(BF16)
 
     n63 = pl.ds(0, NG * GW - 1)
-    await_bytes(v1.at[n63], snd.at[0])
-    await_bytes(r1.at[pl.ds(0, 3)], snd.at[1])
-    await_bytes(r2.at[n63], snd.at[2])
-    await_bytes(s3.at[n63], snd.at[3])
-    await_bytes(rs.at[pl.ds(0, 2)], snd.at[4])
-    await_bytes(zs, snd.at[5])
-    await_bytes(s4.at[n63], snd.at[6])
+    await_bytes(v1.at[pl.ds(0, 62)], snd.at[0])
+    await_bytes(rs.at[pl.ds(0, 3), :, 0], snd.at[1])
+    await_bytes(rs.at[pl.ds(0, 2)], snd.at[2])
+    await_bytes(r2.at[n63], snd.at[3])
+    await_bytes(s3.at[n63], snd.at[4])
+    await_bytes(rs.at[pl.ds(0, 2)], snd.at[5])
+    await_bytes(zr, snd.at[6])
+    await_bytes(r4.at[pl.ds(0, 62)], snd.at[7])
 
 
 def spectra_loop(focus, kern, tile_mask, onset2, fwd, fwdt, invt):
@@ -362,22 +395,24 @@
             pltpu.VMEM((1536, 128), F32),
             pltpu.VMEM((1536, 128), F32),
             pltpu.VMEM((64, *chunk), BF16),
-            pltpu.VMEM((4, 64, *chunk), BF16),
-            pltpu.VMEM((3072, 256), BF16),
+            pltpu.VMEM((32, *chunk), BF16),
+            pltpu.VMEM((4, NG, 2, 8, *chunk), BF16),
+            pltpu.VMEM((768, 256), BF16),
+            pltpu.VMEM((NG, 384, 256), F32),
             pltpu.VMEM((2, 32, *chunk), BF16),
             pltpu.VMEM((64, *chunk), BF16),
             pltpu.VMEM((64, *chunk), BF16),
             pltpu.VMEM((2, 32, *chunk), BF16),
             pltpu.VMEM((256, 768), BF16),
             pltpu.VMEM((768, 256), F32),
-            pltpu.VMEM((4, 64, *chunk), BF16),
-            pltpu.VMEM((2, 64, *chunk), BF16),
+            pltpu.VMEM((4, NG, 2, 8, *chunk), BF16),
+            pltpu.VMEM((2, NG, 2, 8, *chunk), BF16),
+            pltpu.VMEM((2, NG, 2, 8, *chunk), BF16),
+            pltpu.VMEM((3, NG, 8, *chunk), BF16),
+            pltpu.VMEM((2, NG, 8, *chunk), BF16),
             pltpu.VMEM((64, *chunk), BF16),
-            pltpu.VMEM((64, *chunk), BF16),
-            pltpu.VMEM((64, *chunk), BF16),
-            pltpu.VMEM((64, *chunk), BF16),
-            dma, dma, dma((7,)), dma((NG,)), dma((3, NG)), dma, dma,
-            dma((2, NG)), dma((NG,)), dma, dma,
+            dma, dma, dma((8,)), dma((NG,)), dma((NG,)), dma((3, NG)), dma((4, NG)),
+            dma, dma, dma((2, NG)), dma((3, NG)), dma,
         ],
         compiler_params=pltpu.CompilerParams(
             collective_id=0, has_side_effects=True, vmem_limit_bytes=60 * 1024 * 1024
@@ -388,10 +423,11 @@
 
 def finish_kernel(points, onset_ref, spec_ref, focus_ref, inv_ref, out_ref):
     i = pl.program_id(0)
+    first = lax.axis_index("half") * 32 + i * points
     upd = jnp.dot(spec_ref[...], inv_ref[...], preferred_element_type=F32)
     time = lax.broadcasted_iota(jnp.int32, (48, 512), 1)
     for n in range(points):
-        kept = jnp.where(time < onset_ref[i * points + n], upd[n * 48 : (n + 1) * 48], 0.0)
+        kept = jnp.where(time < onset_ref[first + n], upd[n * 48 : (n + 1) * 48], 0.0)
         out_ref[n] = (focus_ref[n].astype(F32) + kept).astype(BF16)
 
 
@@ -415,16 +451,14 @@
 def shards(focus, kernel, onset, tile_mask):
     own_points, local_receivers, length = focus.shape
     fwd, fwdt, inv, invt = make_tables(64, length)
-    halves = onset.reshape(2, 64)
     spec = spectra_loop(
         focus.reshape(own_points * local_receivers, length),
         kernel[0],
         tile_mask,
-        jnp.concatenate([halves, halves], axis=1),
+        onset.reshape(1, 128),
         fwd, fwdt, invt,
     )
-    mine = lax.dynamic_slice_in_dim(onset, lax.axis_index("half") * own_points, own_points, 0)
-    return finish(mine, spec, focus, inv)
+    return finish(onset, spec, focus, inv)
 
 
 def solution(mesh):

time: 101 us -> 95.7 us (0.948)
  Pallas kernels: 97.9 us -> 95.5 us
  local copies, waits for them, and re-layouts: 2.04 us -> 0 us
    pallas_call x1, Pallas kernels: 93.7 us -> 91.4 us  [spectra_loop(): pl.pallas_call(focus_kernel, out_shape=jax.ShapeDtypeStruct((1536, 128),...]
    dynamic_slice x1 -> x0, local copies, waits for them, and re-layouts: 1.3 us -> none  [shards(): lax.dynamic_slice_in_dim(onset, lax.axis_index('half') * own_points, own_...]
where the time goes in v2:
time: 95.7 us; the launch traced here: 95.6 us
  Pallas kernels  95.5 us (100%)
    pallas_call x1, Pallas kernels, spectra_loop(): pl.pallas_call(focus_kernel, out_shape=jax.ShapeDtypeStruct((1536, 128),...  91.4 us
    pallas_call x1, Pallas kernels, finish(): pl.pallas_call(functools.partial(finish_kernel, points), out_shape=jax.Sh...  4.18 us

profile of v2, /device:TPU:1, one launch (start us, length us, event | category | flops | bytes accessed | tf_op | source)
XLA Modules:
  0.0 95.6 jit_solution(10549027880198642248)
XLA Ops:
  0.0 91.4 %focus_update.1.spec_ref = bf16[1536,128]{1,0:T(8,128)(2,1)} custom-call(bf16[1536,512]{1,0:T(8,128)(2,1)} %bitcast.4, bf16[2,768,3072]{2,1,0:T(8,128)(2,1)} %bitcast.3, s32[12,12]{1,0:T(8,128)} %mask_ref.1, s32[1,128]{1,0:T(1,128)} %bitcast.5, bf16[512,128]{1,0:T(8,128)(2,1)} %constant.8.fwd_ref, bf16[128,512]{1,0:T(8,128)(2,1)} %constant.9.fwdt_ref, ...), custom_call_target="tpu_custom_call" | custom-call | tf_op jit(solution)/shard_map/focus_update/pallas_call | solution.py:387
  91.4 4.2 %finish.1 = bf16[32,48,512]{2,1,0:T(8,128)(2,1)} custom-call(s32[128]{0:T(128)} %onset_ref.1, bf16[1536,128]{1,0:T(8,128)(2,1)} %focus_update.1.spec_ref, bf16[32,48,512]{2,1,0:T(8,128)(2,1)} %focus_ref.1, bf16[128,512]{1,0:T(8,128)(2,1)} %constant.11.inv_ref), custom_call_target="tpu_custom_call" | custom-call | tf_op jit(solution)/shard_map/finish/pallas_call | solution.py:436

commit v3 on v2

--- a/solution.py
+++ b/solution.py
@@ -28,12 +28,17 @@
     return fwd, fwd.T, invt.T, invt
 
 
+def z_step(n):
+    m = lax.div(n, 2)
+    return jnp.where(n < 2, 4 * n, jnp.where(lax.rem(n, 2) == 0, m, 8 - m))
+
+
 def wide_peer(me, d):
     x, loc = lax.div(me, GW), lax.rem(me, GW)
     i, n = lax.div(d, GW), lax.rem(d, GW)
     z, y = lax.div(loc, 2), lax.rem(loc, 2)
     tx = lax.rem(x + i, NG)
-    tz = lax.rem(z + lax.div(n, 2), 8)
+    tz = lax.rem(z + z_step(lax.div(n, 2)), 8)
     ty = lax.rem(y + lax.rem(n, 2), 2)
     return tx * GW + tz * 2 + ty
 
@@ -54,10 +59,10 @@
 
 
 def focus_kernel(
-    focus_hbm, kern_hbm, mask_ref, onset_ref, fwd_ref, fwdt_ref, invt_ref,
+    focus_hbm, kern_hbm, mask_ref, onset_hbm, onset_smem, fwd_hbm, fwdt_hbm, inv_hbm, invt_hbm,
     out_ref,
-    xv, mv, big, tr, v1, b1, r1, fv, acc, s2, r2, s3, h3, ht, pv, rs, qv, zs, zr, s4, r4,
-    sem_x, sem_m, snd, rcva, rcvb, rel, chip, rcv2, rcv3, rcvq, rcvz, rcv4,
+    onset_ref, fwd_ref, fwdt_ref, inv_ref, invt_ref, xv, mv, big, tr, v1, b1, r1, fv, acc, s2, r2, s3, h3, ht, pv, rs, qv, zs, zr, s4, r4,
+    sem_t, sem_x, sem_m, snd, first, rcva, rcvb, rel, chip, rcv2, rcv3, rcvq, rcvz, rcv4,
 ):
     me = lax.axis_index("wide")
     hf = lax.axis_index("half")
@@ -67,10 +72,6 @@
     ypeer = (1 - yh) * 2 + q
     z, yl = lax.div(lax.rem(me, GW), 2), lax.rem(me, 2)
     beside = x * GW + 2 * z + (1 - yl)
-    copy_x = pltpu.make_async_copy(focus_hbm, xv, sem_x)
-    copy_x.start()
-    copy_m = pltpu.make_async_copy(kern_hbm, mv, sem_m)
-    copy_m.start()
     barrier = pltpu.get_barrier_semaphore()
 
     @pl.loop(1, NG * GW)
@@ -90,25 +91,43 @@
             device_id_type=pl.DeviceIdType.MESH,
         )
 
+    tables = [
+        pltpu.make_async_copy(src, dst, sem_t.at[n])
+        for n, (src, dst) in enumerate(
+            (
+                (fwd_hbm, fwd_ref), (fwdt_hbm, fwdt_ref), (inv_hbm, inv_ref),
+                (invt_hbm, invt_ref), (onset_hbm, onset_ref),
+            )
+        )
+    ]
+    tables[0].start()
+    copy_x = pltpu.make_async_copy(focus_hbm, xv, sem_x)
+    copy_x.start()
+    copy_m = pltpu.make_async_copy(kern_hbm, mv, sem_m)
+    copy_m.start()
+    for table in tables[1:]:
+        table.start()
+
     lane = lax.broadcasted_iota(jnp.int32, (1, 128), 1)
     low64 = lane < 64
     low32 = lax.rem(lane, 64) < 32
 
+    tables[0].wait()
     copy_x.wait()
     for b in range(4):
         rows = pl.ds(b * 384, 384)
         big[rows, :] = jnp.dot(xv[rows, :], fwd_ref[...], preferred_element_type=F32)
 
-    @pl.loop(0, 12)
+    @pl.loop(0, 12, unroll=4)
     def _(jp):
         j = 2 * jp
         a = [
             [big[pl.ds(s * CH + j + jj, 32, stride=48), :] for jj in range(2)]
             for s in range(2)
         ]
-        first = [jnp.where(low64, a[s][0], pltpu.roll(a[s][1], 64, 1)) for s in range(2)]
-        second = [jnp.where(low64, pltpu.roll(a[s][0], 64, 1), a[s][1]) for s in range(2)]
-        t = jnp.concatenate(first + second, axis=0).T
+        even = [jnp.where(low64, a[s][0], pltpu.roll(a[s][1], 64, 1)) for s in range(2)]
+        odd = [jnp.where(low64, pltpu.roll(a[s][0], 64, 1), a[s][1]) for s in range(2)]
+        t = jnp.concatenate(even + odd, axis=0).T
         tr[pl.ds(j, 64, stride=CH), :] = t[:64]
         tr[pl.ds(j + 1, 64, stride=CH), :] = t[64:]
 
@@ -122,27 +141,36 @@
     pltpu.make_async_copy(v1.at[me], r1.at[hf, x, yl, z], rcva.at[x]).start()
     pltpu.make_async_copy(v1.at[own_k + 1 - yl], b1.at[here], rcvb.at[x]).start()
 
-    @pl.loop(1, 32)
-    def _(d):
-        tx = lax.rem(x + lax.div(d, 8), NG)
-        tz = lax.rem(z + lax.rem(d, 8), 8)
-        k = tx * GW + tz * 2
-        peer = k + yl
-        send(v1.at[peer], r1.at[hf, x, yl, z], snd.at[0], rcva.at[x], peer, hf)
-        send(v1.at[k + 1 - yl], b1.at[here], snd.at[0], rcvb.at[x], peer, hf)
-
-    copy_m.wait()
-
-    @pl.loop(0, 36)
-    def _(n):
-        a, b = lax.div(n, 12), lax.rem(n, 12)
-        keep = mask_ref[hf * 3 + a, b].astype(F32)
-        keep = jnp.full((TILE, TILE), keep, F32).astype(BF16)
-        rows = pl.ds(pl.multiple_of(a * TILE, TILE), TILE)
-        cols = pl.ds(pl.multiple_of(b * TILE, TILE), TILE)
-        for c in range(2):
-            mv[c, rows, cols] = mv[c, rows, cols] * keep
-
+    for i in range(NG):
+        tx = lax.rem(x + i, NG)
+
+        @pl.loop(1 if i == 0 else 0, 8)
+        def _(n):
+            tz = lax.rem(z + z_step(n), 8)
+            k = tx * GW + tz * 2
+            peer = k + yl
+            send(v1.at[peer], r1.at[hf, x, yl, z], first.at[i], rcva.at[x], peer, hf)
+            send(v1.at[k + 1 - yl], b1.at[here], first.at[i], rcvb.at[x], peer, hf)
+
+        if i == 0:
+            copy_m.wait()
+        if i < 3:
+
+            @pl.loop(12 * i, 12 * (i + 1))
+            def _(n):
+                b = n - 12 * i
+                keep = mask_ref[hf * 3 + i, b].astype(F32)
+                keep = jnp.full((TILE, TILE), keep, F32).astype(BF16)
+                rows = pl.ds(i * TILE, TILE)
+                cols = pl.ds(pl.multiple_of(b * TILE, TILE), TILE)
+                for c in range(2):
+                    mv[c, rows, cols] = mv[c, rows, cols] * keep
+
+        if i >= 1:
+            await_bytes(v1.at[pl.ds(0, 14 if i == 1 else 16)], first.at[i - 1])
+
+    for table in tables[1:]:
+        table.wait()
     acc[...] = jnp.zeros_like(acc)
     sign = jnp.where(low64, -1.0, 1.0).astype(F32)
 
@@ -155,48 +183,50 @@
         lhs = jnp.concatenate([mv[0, rows, cols], mv[1, rows, cols]], axis=0)
         return jnp.dot(lhs, fv[...], preferred_element_type=F32)
 
-    @pl.loop(0, NG + 2)
+    @pl.loop(0, NG)
+    def _(i):
+        g = lax.rem(x - i + NG, NG)
+        own = r1.at[hf, g, yl]
+        await_bytes(own, rcva.at[g])
+        send(own, own, snd.at[1], rel.at[0, g], me, ypeer)
+        await_bytes(b1.at[slab(g)], rcvb.at[g])
+        send(b1.at[slab(g)], own, snd.at[1], rel.at[1, g], beside, hf)
+        send(b1.at[slab(g)], own, snd.at[1], rel.at[2, g], beside, ypeer)
+        send(own, own, snd.at[2], chip.at[0, g], me, partner)
+
+    @pl.loop(0, NG + 1)
     def _(i):
         @pl.when(i < NG)
         def _():
             g = lax.rem(x - i + NG, NG)
-            own = r1.at[hf, g, yl]
-            await_bytes(own, rcva.at[g])
-            send(own, own, snd.at[1], rel.at[0, g], me, ypeer)
-            send(own, own, snd.at[2], chip.at[0, g], me, partner)
-            await_bytes(b1.at[slab(g)], rcvb.at[g])
-            send(b1.at[slab(g)], own, snd.at[1], rel.at[1, g], beside, hf)
-            send(b1.at[slab(g)], own, snd.at[1], rel.at[2, g], beside, ypeer)
-
-        @pl.when(jnp.logical_and(i >= 1, i <= NG))
-        def _():
-            g = lax.rem(x - i + 1 + NG, NG)
             for n, (h, y) in enumerate(((ypeer, yl), (hf, 1 - yl), (ypeer, 1 - yl))):
                 got = r1.at[h, g, y]
                 await_bytes(got, rel.at[n, g])
                 send(got, got, snd.at[2], chip.at[n + 1, g], me, partner)
 
-        @pl.when(i >= 2)
+        @pl.when(i >= 1)
         def _():
-            g = lax.rem(x - i + 2 + NG, NG)
+            g = lax.rem(x - i + 1 + NG, NG)
             diag = (1 - yh) * 2 + (1 - q)
             for n, (h, y) in enumerate(
                 ((partner, yl), (diag, yl), (partner, 1 - yl), (diag, 1 - yl))
             ):
                 await_bytes(r1.at[h, g, y], chip.at[n, g])
 
-            @pl.loop(0, GW)
-            def _(n):
-                at = (lax.rem(n, 2), lax.div(n, 2))
-                rows = pl.ds(pl.multiple_of(n * 48, 48), 48)
-                for t in range(2):
-                    b0 = r1[2 * t, g, at[0], at[1]].astype(F32)
-                    b1_ = r1[2 * t + 1, g, at[0], at[1]].astype(F32)
+            for t in range(2):
+                for y in range(2):
+                    b0 = r1[2 * t, g, y].astype(F32).reshape(192, 128)
+                    b1_ = r1[2 * t + 1, g, y].astype(F32).reshape(192, 128)
                     o0 = jnp.where(low32, b0, pltpu.roll(b1_, 32, 1))
                     o1 = jnp.where(low32, pltpu.roll(b0, 96, 1), b1_)
-                    fv[rows, t * 128 : (t + 1) * 128] = jnp.concatenate([o0, o1], axis=0).astype(BF16)
-
-            @pl.when(i < NG + 1)
+                    for zz in range(8):
+                        at = slice(zz * CH, (zz + 1) * CH)
+                        rows = (zz * 2 + y) * 48
+                        fv[rows : rows + 48, t * 128 : (t + 1) * 128] = jnp.concatenate(
+                            [o0[at], o1[at]], axis=0
+                        ).astype(BF16)
+
+            @pl.when(i < NG)
             def _():
                 @pl.loop(0, NG)
                 def _(b):
@@ -237,7 +267,7 @@
     mute = lax.broadcasted_iota(jnp.int32, (512, 128), 0) < mine
     mute = jnp.concatenate([mute, mute], axis=1)
 
-    @pl.loop(0, 6)
+    @pl.loop(0, 6, unroll=3)
     def _(rq):
         cols = []
         for u in range(2):
@@ -278,7 +308,7 @@
                     piece[u * 128 : (u + 1) * 128].T.astype(BF16)
                 )
 
-    @pl.loop(0, NG + 2)
+    @pl.loop(0, NG + 1)
     def _(i):
         @pl.when(i < NG)
         def _():
@@ -298,20 +328,30 @@
                 )
                 pv[b * TILE : (b + 1) * TILE, :] = pc.T
 
-            @pl.loop(0, GW)
-            def _(n):
-                y, zz = lax.rem(n, 2), lax.div(n, 2)
-                for t in range(2):
-                    base = pl.multiple_of(n * 48, 8)
-                    i0 = pv[pl.ds(base, CH), t * 128 : (t + 1) * 128]
-                    i1 = pv[pl.ds(pl.multiple_of(base + CH, 8), CH), t * 128 : (t + 1) * 128]
-                    rs[2 * t, g, y, zz] = jnp.where(low32, i0, pltpu.roll(i1, 32, 1)).astype(BF16)
-                    rs[2 * t + 1, g, y, zz] = jnp.where(low32, pltpu.roll(i0, 96, 1), i1).astype(BF16)
+            for t in range(2):
+                for y in range(2):
+                    i0, i1 = [
+                        jnp.concatenate(
+                            [
+                                pv[
+                                    (zz * 2 + y) * 48 + u * CH : (zz * 2 + y) * 48 + (u + 1) * CH,
+                                    t * 128 : (t + 1) * 128,
+                                ]
+                                for zz in range(8)
+                            ],
+                            axis=0,
+                        )
+                        for u in range(2)
+                    ]
+                    o0 = jnp.where(low32, i0, pltpu.roll(i1, 32, 1)).astype(BF16)
+                    o1 = jnp.where(low32, pltpu.roll(i0, 96, 1), i1).astype(BF16)
+                    rs[2 * t, g, y] = o0.reshape(8, CH, 128)
+                    rs[2 * t + 1, g, y] = o1.reshape(8, CH, 128)
 
             for t in range(2):
                 send(rs.at[2 * t + (1 - q), g], qv.at[t, g], snd.at[5], rcvq.at[t, g], me, partner)
 
-        @pl.when(jnp.logical_and(i >= 1, i <= NG))
+        @pl.when(i >= 1)
         def _():
             g = lax.rem(x + i - 1, NG)
             for t in range(2):
@@ -322,36 +362,36 @@
             send(zs.at[yh, g, 1 - yl], zr.at[1, g], snd.at[6], rcvz.at[1, g], beside, hf)
             send(zs.at[1 - yh, g, yl], zr.at[0, g], snd.at[6], rcvz.at[0, g], me, ypeer)
 
-        @pl.when(i >= 2)
-        def _():
-            g = lax.rem(x + i - 2, NG)
-            for n in range(3):
-                await_bytes(zr.at[n, g], rcvz.at[n, g])
-            s4[yl, g] = (zs[yh, g, yl].astype(F32) + zr[0, g].astype(F32)).astype(BF16)
-            s4[1 - yl, g] = (zr[1, g].astype(F32) + zr[2, g].astype(F32)).astype(BF16)
-
-            @pl.loop(0, 8)
-            def _(n):
-                tz = lax.rem(z + n, 8)
-                peer = g * GW + tz * 2 + yl
-                k = x * GW + z * 2
-
-                @pl.when(i - 2 + n > 0)
-                def _():
-                    send(s4.at[0, g, tz], r4.at[k], snd.at[7], rcv4, peer, hf)
-                    send(s4.at[1, g, tz], r4.at[k + 1], snd.at[7], rcv4, peer, hf)
-
-                @pl.when(i - 2 + n == 0)
-                def _():
-                    pltpu.make_async_copy(s4.at[0, g, tz], r4.at[k], rcv4).start()
-                    pltpu.make_async_copy(s4.at[1, g, tz], r4.at[k + 1], rcv4).start()
+    @pl.loop(0, NG)
+    def _(i):
+        g = lax.rem(x + i, NG)
+        for n in range(3):
+            await_bytes(zr.at[n, g], rcvz.at[n, g])
+        s4[yl, g] = (zs[yh, g, yl].astype(F32) + zr[0, g].astype(F32)).astype(BF16)
+        s4[1 - yl, g] = (zr[1, g].astype(F32) + zr[2, g].astype(F32)).astype(BF16)
+
+        @pl.loop(0, 8)
+        def _(n):
+            tz = lax.rem(z + z_step(n), 8)
+            peer = g * GW + tz * 2 + yl
+            k = x * GW + z * 2
+
+            @pl.when(i + n > 0)
+            def _():
+                send(s4.at[0, g, tz], r4.at[k], snd.at[7], rcv4, peer, hf)
+                send(s4.at[1, g, tz], r4.at[k + 1], snd.at[7], rcv4, peer, hf)
+
+            @pl.when(i + n == 0)
+            def _():
+                pltpu.make_async_copy(s4.at[0, g, tz], r4.at[k], rcv4).start()
+                pltpu.make_async_copy(s4.at[1, g, tz], r4.at[k + 1], rcv4).start()
 
     await_bytes(r4, rcv4)
 
     for b in range(4):
         big[pl.ds(b * 384, 384), :] = r4[pl.ds(b * 16, 16)].astype(F32).reshape(384, 128)
 
-    @pl.loop(0, 12)
+    @pl.loop(0, 12, unroll=4)
     def _(jp):
         j = 2 * jp
         a0 = big[pl.ds(j, 64, stride=CH), :]
@@ -363,12 +403,18 @@
             tr[pl.ds(s * CH + j, 32, stride=48), :] = l0[s * 32 : (s + 1) * 32]
             tr[pl.ds(s * CH + j + 1, 32, stride=48), :] = l1[s * 32 : (s + 1) * 32]
 
-    for b in range(4):
-        rows = pl.ds(b * 384, 384)
-        out_ref[rows, :] = tr[rows, :].astype(BF16)
+    time = lax.broadcasted_iota(jnp.int32, (48, 512), 1)
+    for b in range(4):
+        upd = jnp.dot(
+            tr[pl.ds(b * 384, 384), :].astype(BF16), inv_ref[...], preferred_element_type=F32
+        )
+        for n in range(8):
+            rows = pl.ds((b * 8 + n) * 48, 48)
+            kept = jnp.where(time < onset_smem[hf * 32 + b * 8 + n], upd[n * 48 : (n + 1) * 48], 0.0)
+            out_ref[rows, :] = (xv[rows, :].astype(F32) + kept).astype(BF16)
 
     n63 = pl.ds(0, NG * GW - 1)
-    await_bytes(v1.at[pl.ds(0, 62)], snd.at[0])
+    await_bytes(v1.at[pl.ds(0, 16)], first.at[NG - 1])
     await_bytes(rs.at[pl.ds(0, 3), :, 0], snd.at[1])
     await_bytes(rs.at[pl.ds(0, 2)], snd.at[2])
     await_bytes(r2.at[n63], snd.at[3])
@@ -378,7 +424,7 @@
     await_bytes(r4.at[pl.ds(0, 62)], snd.at[7])
 
 
-def spectra_loop(focus, kern, tile_mask, onset2, fwd, fwdt, invt):
+def focus_update(focus, kern, tile_mask, onset, points, fwd, fwdt, inv, invt):
     dma = pltpu.SemaphoreType.DMA
     vmem = pl.BlockSpec(memory_space=pltpu.VMEM)
     hbm = pl.BlockSpec(memory_space=pl.ANY)
@@ -386,10 +432,15 @@
     chunk = (CH, 128)
     return pl.pallas_call(
         focus_kernel,
-        out_shape=jax.ShapeDtypeStruct((1536, 128), BF16),
-        in_specs=[hbm, hbm, smem, vmem, vmem, vmem, vmem],
+        out_shape=pltpu.VMEM((1536, 512), BF16),
+        in_specs=[hbm, hbm, smem, hbm, smem, hbm, hbm, hbm, hbm],
         out_specs=vmem,
         scratch_shapes=[
+            pltpu.VMEM((1, 128), jnp.int32),
+            pltpu.VMEM((512, 128), BF16),
+            pltpu.VMEM((128, 512), BF16),
+            pltpu.VMEM((128, 512), BF16),
+            pltpu.VMEM((512, 128), BF16),
             pltpu.VMEM((1536, 512), BF16),
             pltpu.VMEM((2, 768, 3072), BF16),
             pltpu.VMEM((1536, 128), F32),
@@ -411,54 +462,25 @@
             pltpu.VMEM((3, NG, 8, *chunk), BF16),
             pltpu.VMEM((2, NG, 8, *chunk), BF16),
             pltpu.VMEM((64, *chunk), BF16),
-            dma, dma, dma((8,)), dma((NG,)), dma((NG,)), dma((3, NG)), dma((4, NG)),
+            dma((5,)), dma, dma, dma((8,)), dma((NG,)), dma((NG,)), dma((NG,)), dma((3, NG)), dma((4, NG)),
             dma, dma, dma((2, NG)), dma((3, NG)), dma,
         ],
         compiler_params=pltpu.CompilerParams(
-            collective_id=0, has_side_effects=True, vmem_limit_bytes=60 * 1024 * 1024
+            collective_id=0, has_side_effects=True, vmem_limit_bytes=50 * 1024 * 1024
         ),
         name="focus_update",
-    )(focus, kern, tile_mask, onset2, fwd, fwdt, invt)
-
-
-def finish_kernel(points, onset_ref, spec_ref, focus_ref, inv_ref, out_ref):
-    i = pl.program_id(0)
-    first = lax.axis_index("half") * 32 + i * points
-    upd = jnp.dot(spec_ref[...], inv_ref[...], preferred_element_type=F32)
-    time = lax.broadcasted_iota(jnp.int32, (48, 512), 1)
-    for n in range(points):
-        kept = jnp.where(time < onset_ref[first + n], upd[n * 48 : (n + 1) * 48], 0.0)
-        out_ref[n] = (focus_ref[n].astype(F32) + kept).astype(BF16)
-
-
-def finish(onset, spec, focus, inv):
-    points = 8
-    return pl.pallas_call(
-        functools.partial(finish_kernel, points),
-        out_shape=jax.ShapeDtypeStruct(focus.shape, BF16),
-        grid=(32 // points,),
-        in_specs=[
-            pl.BlockSpec(memory_space=pltpu.SMEM),
-            pl.BlockSpec((points * 48, 128), lambda i: (i, 0)),
-            pl.BlockSpec((points, 48, 512), lambda i: (i, 0, 0)),
-            pl.BlockSpec((128, 512), lambda i: (0, 0)),
-        ],
-        out_specs=pl.BlockSpec((points, 48, 512), lambda i: (i, 0, 0)),
-        name="finish",
-    )(onset, spec, focus, inv)
+    )(focus, kern, tile_mask, onset, points, fwd, fwdt, inv, invt)
 
 
 def shards(focus, kernel, onset, tile_mask):
     own_points, local_receivers, length = focus.shape
     fwd, fwdt, inv, invt = make_tables(64, length)
-    spec = spectra_loop(
-        focus.reshape(own_points * local_receivers, length),
-        kernel[0],
-        tile_mask,
-        onset.reshape(1, 128),
-        fwd, fwdt, invt,
+    pinned = functools.partial(pltpu.with_memory_space_constraint, memory_space=pltpu.HBM)
+    out = focus_update(
+        pinned(focus.reshape(own_points * local_receivers, length)),
+        pinned(kernel[0]), pinned(tile_mask), pinned(onset.reshape(1, 128)), onset, *map(pinned, (fwd, fwdt, inv, invt)),
     )
-    return finish(onset, spec, focus, inv)
+    return out.reshape(focus.shape)
 
 
 def solution(mesh):

time: 95.7 us -> 83 us (0.87)
  Pallas kernels: 95.5 us -> 81.8 us
  local copies, waits for them, and re-layouts: 0 us -> 1.15 us
    pallas_call x2 -> x1, Pallas kernels: 95.5 us -> 81.8 us  [focus_update(): pl.pallas_call(focus_kernel, out_shape=pltpu.VMEM((1536, 512), BF16), in_...]
    unnamed x0 -> x1, local copies, waits for them, and re-layouts: none -> 1.15 us
where the time goes in v3:
time: 83 us; the launch traced here: 82.9 us
  Pallas kernels  81.8 us (99%)
  local copies, waits for them, and re-layouts  1.15 us (1%)
    pallas_call x1, Pallas kernels, focus_update(): pl.pallas_call(focus_kernel, out_shape=pltpu.VMEM((1536, 512), BF16), in_...  81.8 us

profile of v3, /device:TPU:1, one launch (start us, length us, event | category | flops | bytes accessed | tf_op | source)
XLA Modules:
  0.0 82.9 jit_solution(9016094012315221655)
XLA Ops:
  0.0 81.8 %focus_update.1 = bf16[1536,512]{1,0:T(8,128)(2,1)S(1)} custom-call(bf16[1536,512]{1,0:T(8,128)(2,1)} %bitcast.6, bf16[2,768,3072]{2,1,0:T(8,128)(2,1)} %bitcast.5, s32[12,12]{1,0:T(8,128)} %mask_ref.1, s32[1,128]{1,0:T(1,128)} %bitcast.7, s32[128]{0:T(128)} %onset_smem.1, bf16[512,128]{1,0:T(8,128)(2,1)} %constant.8.fwd_hbm, ...), custom_call_target="tpu_custom_call" | custom-call | tf_op jit(solution)/shard_map/focus_update/pallas_call | solution.py:433
  81.8 1.1 %copy.8 = bf16[32,48,512]{2,1,0:T(8,128)(2,1)} copy(bf16[32,48,512]{2,1,0:T(8,128)(2,1)S(1)} %bitcast.4) | data formatting | bytes 3145728

commit v4 on v3

--- a/solution.py
+++ b/solution.py
@@ -61,7 +61,7 @@
 def focus_kernel(
     focus_hbm, kern_hbm, mask_ref, onset_hbm, onset_smem, fwd_hbm, fwdt_hbm, inv_hbm, invt_hbm,
     out_ref,
-    onset_ref, fwd_ref, fwdt_ref, inv_ref, invt_ref, xv, mv, big, tr, v1, b1, r1, fv, acc, s2, r2, s3, h3, ht, pv, rs, qv, zs, zr, s4, r4,
+    onset_ref, fwd_ref, fwdt_ref, inv_ref, invt_ref, xv, mv, big, tr, v1, b1, r1, fv, acc, s2a, s2b, r2a, r2b, s3a, s3b, h3a, h3b, ht, pv, rs, qv, zs, zr, s4, r4,
     sem_t, sem_x, sem_m, snd, first, rcva, rcvb, rel, chip, rcv2, rcv3, rcvq, rcvz, rcv4,
 ):
     me = lax.axis_index("wide")
@@ -178,7 +178,7 @@
         return pl.ds(g * 8, 8)
 
     def product(g, b):
-        rows = pl.ds(pl.multiple_of(b * 192, 192), 192)
+        rows = pl.ds(pl.multiple_of(b * TILE, TILE), TILE)
         cols = pl.ds(pl.multiple_of(g * 768, 768), 768)
         lhs = jnp.concatenate([mv[0, rows, cols], mv[1, rows, cols]], axis=0)
         return jnp.dot(lhs, fv[...], preferred_element_type=F32)
@@ -228,37 +228,61 @@
 
             @pl.when(i < NG)
             def _():
-                @pl.loop(0, NG)
+                @pl.loop(0, 3)
                 def _(b):
                     acc[b] += product(g, b)
 
-    @pl.loop(0, NG)
+    def waves(b):
+        full = acc[b] + product(lax.rem(x + 1, NG), b)
+        return [
+            (
+                full[:TILE, t * 128 : (t + 1) * 128]
+                + sign * pltpu.roll(full[TILE:, t * 128 : (t + 1) * 128], 64, 1)
+            ).astype(BF16)
+            for t in range(2)
+        ]
+
+    def spread(first, last, src_of, dst, ssem, rsem):
+        @pl.loop(first, last)
+        def _(d):
+            peer = wide_peer(me, d)
+
+            @pl.when(d > 0)
+            def _():
+                send(src_of(peer), dst, ssem, rsem, peer, hf)
+
+            @pl.when(d == 0)
+            def _():
+                pltpu.make_async_copy(src_of(peer), dst, rsem).start()
+
+    def by_row(ref):
+        return lambda peer: ref.at[lax.rem(peer, 2), lax.div(peer, 2)]
+
+    @pl.loop(0, 2)
     def _(i):
-        b = lax.rem(x + i, NG)
-        full = acc[b] + product(lax.rem(x + 1, NG), b)
-        for t in range(2):
-            re = full[:192, t * 128 : (t + 1) * 128]
-            im = full[192:, t * 128 : (t + 1) * 128]
-            wv = re + sign * pltpu.roll(im, 64, 1)
-            s2[t, pl.ds(b * 8, 8)] = wv.astype(BF16).reshape(8, CH, 128)
-
-        @pl.loop(0, GW)
+        b = lax.rem(lax.div(x, 2) + i, 2)
+        for t, wv in enumerate(waves(b)):
+            s2a[t, pl.ds(b * 16, 16)] = wv.reshape(16, 16, 128)
+
+        @pl.loop(0, 32)
         def _(n):
-            peer = wide_peer(me, i * GW + n)
-            src = s2.at[lax.rem(peer, 2), lax.div(peer, 2)]
+            tx = 2 * b + lax.rem(lax.rem(x, 2) + lax.div(n, GW), 2)
+            peer = tx * GW + lax.rem(wide_peer(me, n), GW)
 
             @pl.when(i + n > 0)
             def _():
-                send(src, r2.at[me], snd.at[3], rcv2, peer, hf)
+                send(by_row(s2a)(peer), r2a.at[me], snd.at[3], rcv2.at[0], peer, hf)
 
             @pl.when(i + n == 0)
             def _():
-                pltpu.make_async_copy(src, r2.at[me], rcv2).start()
-
-    await_bytes(r2, rcv2)
-
-    for b in range(4):
-        big[pl.ds(b * 384, 384), :] = r2[pl.ds(b * 16, 16)].astype(F32).reshape(384, 128)
+                pltpu.make_async_copy(by_row(s2a)(peer), r2a.at[me], rcv2.at[0]).start()
+
+    for t, wv in enumerate(waves(2)):
+        s2b[t] = wv.reshape(32, 8, 128)
+    n63 = pl.ds(0, NG * GW - 1)
+    await_bytes(r2a.at[n63], snd.at[3])
+    spread(0, NG * GW, by_row(s2b), r2b.at[me], snd.at[8], rcv2.at[1])
+
     points = jnp.broadcast_to(onset_ref[...], (8, 128))
     other = pltpu.roll(points, 64, 1)
     mine = jnp.where(
@@ -267,13 +291,17 @@
     mute = lax.broadcasted_iota(jnp.int32, (512, 128), 0) < mine
     mute = jnp.concatenate([mute, mute], axis=1)
 
-    @pl.loop(0, 6, unroll=3)
-    def _(rq):
+    def time_domain(base, count):
+        @pl.loop(0, count // 4, unroll=2)
+        def _(rq):
+            time_step(base + rq * 4, count)
+
+    def time_step(base, count):
         cols = []
         for u in range(2):
-            r = rq * 4 + u * 2
-            a0 = big[pl.ds(r, 64, stride=CH), :]
-            a1 = big[pl.ds(r + 1, 64, stride=CH), :]
+            r = base + u * 2
+            a0 = big[pl.ds(r, 64, stride=count), :]
+            a1 = big[pl.ds(r + 1, 64, stride=count), :]
             top = jnp.where(low64, a0, pltpu.roll(a1, 64, 1))
             bot = jnp.where(low64, pltpu.roll(a0, 64, 1), a1)
             cols.append(jnp.concatenate([top, bot], axis=0))
@@ -282,31 +310,34 @@
         muted = jnp.where(mute, trace, 0.0).astype(BF16)
         back = jnp.dot(fwdt_ref[...], muted, preferred_element_type=F32)
         for u in range(2):
-            r = rq * 4 + u * 2
+            r = base + u * 2
             top = back[:64, u * 128 : (u + 1) * 128]
             bot = back[64:, u * 128 : (u + 1) * 128]
-            tr[pl.ds(r, 64, stride=CH), :] = jnp.where(low64, top, pltpu.roll(bot, 64, 1))
-            tr[pl.ds(r + 1, 64, stride=CH), :] = jnp.where(low64, pltpu.roll(top, 64, 1), bot)
-
-    for b in range(4):
-        s3[pl.ds(b * 16, 16)] = tr[pl.ds(b * 384, 384), :].astype(BF16).reshape(16, CH, 128)
+            tr[pl.ds(r, 64, stride=count), :] = jnp.where(low64, top, pltpu.roll(bot, 64, 1))
+            tr[pl.ds(r + 1, 64, stride=count), :] = jnp.where(low64, pltpu.roll(top, 64, 1), bot)
+
     slot = (lax.rem(me, 2), lax.div(me, 2))
-    pltpu.make_async_copy(s3.at[me], h3.at[slot], rcv3).start()
-
-    @pl.loop(1, NG * GW)
-    def _(d):
-        peer = wide_peer(me, d)
-        send(s3.at[peer], h3.at[slot], snd.at[4], rcv3, peer, hf)
-
-    await_bytes(h3, rcv3)
-
+    await_bytes(r2a, rcv2.at[0])
+    big[0:1024, :] = r2a[...].astype(F32).reshape(1024, 128)
+    time_domain(0, 16)
+    s3a[...] = tr[0:1024, :].astype(BF16).reshape(64, 16, 128)
+    spread(0, NG * GW, lambda peer: s3a.at[peer], h3a.at[slot], snd.at[4], rcv3.at[0])
+    await_bytes(r2b, rcv2.at[1])
+    big[1024:1536, :] = r2b[...].astype(F32).reshape(512, 128)
+    time_domain(1024, 8)
+    s3b[...] = tr[1024:1536, :].astype(BF16).reshape(64, 8, 128)
+    spread(0, NG * GW, lambda peer: s3b.at[peer], h3b.at[slot], snd.at[9], rcv3.at[1])
+
+    await_bytes(h3a, rcv3.at[0])
     for t in range(2):
-        for b in range(2):
-            piece = h3[t, pl.ds(b * 16, 16)].astype(F32).reshape(384, 128)
-            for u in range(3):
-                ht[t * 128 : (t + 1) * 128, b * 384 + u * 128 : b * 384 + (u + 1) * 128] = (
-                    piece[u * 128 : (u + 1) * 128].T.astype(BF16)
-                )
+        for u in range(4):
+            piece = h3a[t, pl.ds(u * 8, 8)].astype(F32).reshape(128, 128)
+            ht[t * 128 : (t + 1) * 128, u * 128 : (u + 1) * 128] = piece.T.astype(BF16)
+    await_bytes(h3b, rcv3.at[1])
+    for t in range(2):
+        for u in range(2):
+            piece = h3b[t, pl.ds(u * 16, 16)].astype(F32).reshape(128, 128)
+            ht[t * 128 : (t + 1) * 128, 512 + u * 128 : 512 + (u + 1) * 128] = piece.T.astype(BF16)
 
     @pl.loop(0, NG + 1)
     def _(i):
@@ -413,12 +444,12 @@
             kept = jnp.where(time < onset_smem[hf * 32 + b * 8 + n], upd[n * 48 : (n + 1) * 48], 0.0)
             out_ref[rows, :] = (xv[rows, :].astype(F32) + kept).astype(BF16)
 
-    n63 = pl.ds(0, NG * GW - 1)
     await_bytes(v1.at[pl.ds(0, 16)], first.at[NG - 1])
     await_bytes(rs.at[pl.ds(0, 3), :, 0], snd.at[1])
     await_bytes(rs.at[pl.ds(0, 2)], snd.at[2])
-    await_bytes(r2.at[n63], snd.at[3])
-    await_bytes(s3.at[n63], snd.at[4])
+    await_bytes(s3a.at[n63], snd.at[4])
+    await_bytes(s3b.at[n63], snd.at[8])
+    await_bytes(s3b.at[n63], snd.at[9])
     await_bytes(rs.at[pl.ds(0, 2)], snd.at[5])
     await_bytes(zr, snd.at[6])
     await_bytes(r4.at[pl.ds(0, 62)], snd.at[7])
@@ -449,11 +480,15 @@
             pltpu.VMEM((32, *chunk), BF16),
             pltpu.VMEM((4, NG, 2, 8, *chunk), BF16),
             pltpu.VMEM((768, 256), BF16),
-            pltpu.VMEM((NG, 384, 256), F32),
-            pltpu.VMEM((2, 32, *chunk), BF16),
-            pltpu.VMEM((64, *chunk), BF16),
-            pltpu.VMEM((64, *chunk), BF16),
-            pltpu.VMEM((2, 32, *chunk), BF16),
+            pltpu.VMEM((3, 512, 256), F32),
+            pltpu.VMEM((2, 32, 16, 128), BF16),
+            pltpu.VMEM((2, 32, 8, 128), BF16),
+            pltpu.VMEM((64, 16, 128), BF16),
+            pltpu.VMEM((64, 8, 128), BF16),
+            pltpu.VMEM((64, 16, 128), BF16),
+            pltpu.VMEM((64, 8, 128), BF16),
+            pltpu.VMEM((2, 32, 16, 128), BF16),
+            pltpu.VMEM((2, 32, 8, 128), BF16),
             pltpu.VMEM((256, 768), BF16),
             pltpu.VMEM((768, 256), F32),
             pltpu.VMEM((4, NG, 2, 8, *chunk), BF16),
@@ -462,8 +497,8 @@
             pltpu.VMEM((3, NG, 8, *chunk), BF16),
             pltpu.VMEM((2, NG, 8, *chunk), BF16),
             pltpu.VMEM((64, *chunk), BF16),
-            dma((5,)), dma, dma, dma((8,)), dma((NG,)), dma((NG,)), dma((NG,)), dma((3, NG)), dma((4, NG)),
-            dma, dma, dma((2, NG)), dma((3, NG)), dma,
+            dma((5,)), dma, dma, dma((10,)), dma((NG,)), dma((NG,)), dma((NG,)), dma((3, NG)), dma((4, NG)),
+            dma((2,)), dma((2,)), dma((2, NG)), dma((3, NG)), dma,
         ],
         compiler_params=pltpu.CompilerParams(
             collective_id=0, has_side_effects=True, vmem_limit_bytes=50 * 1024 * 1024

time: 83 us -> 80.2 us (0.966)
  Pallas kernels: 81.8 us -> 78.9 us
    pallas_call x1, Pallas kernels: 81.8 us -> 78.9 us  [focus_update(): pl.pallas_call(focus_kernel, out_shape=pltpu.VMEM((1536, 512), BF16), in_...]
where the time goes in v4:
time: 80.2 us; the launch traced here: 80.1 us
  Pallas kernels  78.9 us (98%)
  local copies, waits for them, and re-layouts  1.15 us (1%)
    pallas_call x1, Pallas kernels, focus_update(): pl.pallas_call(focus_kernel, out_shape=pltpu.VMEM((1536, 512), BF16), in_...  78.9 us

profile of v4, /device:TPU:1, one launch (start us, length us, event | category | flops | bytes accessed | tf_op | source)
XLA Modules:
  0.0 80.1 jit_solution(6779717577594824364)
XLA Ops:
  0.0 78.9 %focus_update.1 = bf16[1536,512]{1,0:T(8,128)(2,1)S(1)} custom-call(bf16[1536,512]{1,0:T(8,128)(2,1)} %bitcast.6, bf16[2,768,3072]{2,1,0:T(8,128)(2,1)} %bitcast.5, s32[12,12]{1,0:T(8,128)} %mask_ref.1, s32[1,128]{1,0:T(1,128)} %bitcast.7, s32[128]{0:T(128)} %onset_smem.1, bf16[512,128]{1,0:T(8,128)(2,1)} %constant.8.fwd_hbm, ...), custom_call_target="tpu_custom_call" | custom-call | tf_op jit(solution)/shard_map/focus_update/pallas_call | solution.py:464
  78.9 1.1 %copy.8 = bf16[32,48,512]{2,1,0:T(8,128)(2,1)} copy(bf16[32,48,512]{2,1,0:T(8,128)(2,1)S(1)} %bitcast.4) | data formatting | bytes 3145728

commit v5 on v4

--- a/solution.py
+++ b/solution.py
@@ -61,8 +61,8 @@
 def focus_kernel(
     focus_hbm, kern_hbm, mask_ref, onset_hbm, onset_smem, fwd_hbm, fwdt_hbm, inv_hbm, invt_hbm,
     out_ref,
-    onset_ref, fwd_ref, fwdt_ref, inv_ref, invt_ref, xv, mv, big, tr, v1, b1, r1, fv, acc, s2a, s2b, r2a, r2b, s3a, s3b, h3a, h3b, ht, pv, rs, qv, zs, zr, s4, r4,
-    sem_t, sem_x, sem_m, snd, first, rcva, rcvb, rel, chip, rcv2, rcv3, rcvq, rcvz, rcv4,
+    onset_ref, fwd_ref, fwdt_ref, inv_ref, invt_ref, xv, mv, big, tr, v1, b1, r1, fv, acc, s2, r2, s3, h3, ht, pv, rs, qv, zs, zr, s4, r4,
+    sem_t, sem_x, sem_m, snd, first, away, back, rcva, rcvb, rel, chip, rcv2, rcv3, rcvq, rcvz, rcv4,
 ):
     me = lax.axis_index("wide")
     hf = lax.axis_index("half")
@@ -258,30 +258,13 @@
     def by_row(ref):
         return lambda peer: ref.at[lax.rem(peer, 2), lax.div(peer, 2)]
 
-    @pl.loop(0, 2)
-    def _(i):
-        b = lax.rem(lax.div(x, 2) + i, 2)
+    n63 = pl.ds(0, NG * GW - 1)
+    for b in range(3):
         for t, wv in enumerate(waves(b)):
-            s2a[t, pl.ds(b * 16, 16)] = wv.reshape(16, 16, 128)
-
-        @pl.loop(0, 32)
-        def _(n):
-            tx = 2 * b + lax.rem(lax.rem(x, 2) + lax.div(n, GW), 2)
-            peer = tx * GW + lax.rem(wide_peer(me, n), GW)
-
-            @pl.when(i + n > 0)
-            def _():
-                send(by_row(s2a)(peer), r2a.at[me], snd.at[3], rcv2.at[0], peer, hf)
-
-            @pl.when(i + n == 0)
-            def _():
-                pltpu.make_async_copy(by_row(s2a)(peer), r2a.at[me], rcv2.at[0]).start()
-
-    for t, wv in enumerate(waves(2)):
-        s2b[t] = wv.reshape(32, 8, 128)
-    n63 = pl.ds(0, NG * GW - 1)
-    await_bytes(r2a.at[n63], snd.at[3])
-    spread(0, NG * GW, by_row(s2b), r2b.at[me], snd.at[8], rcv2.at[1])
+            s2[b, t] = wv.reshape(32, 8, 128)
+        if b:
+            await_bytes(r2.at[b - 1, n63], away.at[b - 1])
+        spread(0, NG * GW, by_row(s2.at[b]), r2.at[b, me], away.at[b], rcv2.at[b])
 
     points = jnp.broadcast_to(onset_ref[...], (8, 128))
     other = pltpu.roll(points, 64, 1)
@@ -292,8 +275,7 @@
     mute = jnp.concatenate([mute, mute], axis=1)
 
     def time_domain(base, count):
-        @pl.loop(0, count // 4, unroll=2)
-        def _(rq):
+        for rq in range(count // 4):
             time_step(base + rq * 4, count)
 
     def time_step(base, count):
@@ -308,36 +290,30 @@
         spec = jnp.concatenate(cols, axis=1).astype(BF16)
         trace = jnp.dot(invt_ref[...], spec, preferred_element_type=F32)
         muted = jnp.where(mute, trace, 0.0).astype(BF16)
-        back = jnp.dot(fwdt_ref[...], muted, preferred_element_type=F32)
+        again = jnp.dot(fwdt_ref[...], muted, preferred_element_type=F32)
         for u in range(2):
             r = base + u * 2
-            top = back[:64, u * 128 : (u + 1) * 128]
-            bot = back[64:, u * 128 : (u + 1) * 128]
+            top = again[:64, u * 128 : (u + 1) * 128]
+            bot = again[64:, u * 128 : (u + 1) * 128]
             tr[pl.ds(r, 64, stride=count), :] = jnp.where(low64, top, pltpu.roll(bot, 64, 1))
             tr[pl.ds(r + 1, 64, stride=count), :] = jnp.where(low64, pltpu.roll(top, 64, 1), bot)
 
     slot = (lax.rem(me, 2), lax.div(me, 2))
-    await_bytes(r2a, rcv2.at[0])
-    big[0:1024, :] = r2a[...].astype(F32).reshape(1024, 128)
-    time_domain(0, 16)
-    s3a[...] = tr[0:1024, :].astype(BF16).reshape(64, 16, 128)
-    spread(0, NG * GW, lambda peer: s3a.at[peer], h3a.at[slot], snd.at[4], rcv3.at[0])
-    await_bytes(r2b, rcv2.at[1])
-    big[1024:1536, :] = r2b[...].astype(F32).reshape(512, 128)
-    time_domain(1024, 8)
-    s3b[...] = tr[1024:1536, :].astype(BF16).reshape(64, 8, 128)
-    spread(0, NG * GW, lambda peer: s3b.at[peer], h3b.at[slot], snd.at[9], rcv3.at[1])
-
-    await_bytes(h3a, rcv3.at[0])
-    for t in range(2):
-        for u in range(4):
-            piece = h3a[t, pl.ds(u * 8, 8)].astype(F32).reshape(128, 128)
-            ht[t * 128 : (t + 1) * 128, u * 128 : (u + 1) * 128] = piece.T.astype(BF16)
-    await_bytes(h3b, rcv3.at[1])
-    for t in range(2):
-        for u in range(2):
-            piece = h3b[t, pl.ds(u * 16, 16)].astype(F32).reshape(128, 128)
-            ht[t * 128 : (t + 1) * 128, 512 + u * 128 : 512 + (u + 1) * 128] = piece.T.astype(BF16)
+    for b in range(3):
+        rows = pl.ds(b * 512, 512)
+        await_bytes(r2.at[b], rcv2.at[b])
+        big[rows, :] = r2[b].astype(F32).reshape(512, 128)
+        time_domain(b * 512, 8)
+        s3[b] = tr[rows, :].astype(BF16).reshape(64, 8, 128)
+        spread(0, NG * GW, lambda peer: s3.at[b, peer], h3.at[(b, *slot)], back.at[b], rcv3.at[b])
+
+    for b in range(3):
+        await_bytes(h3.at[b], rcv3.at[b])
+        for t in range(2):
+            for u in range(2):
+                piece = h3[b, t, pl.ds(u * 16, 16)].astype(F32).reshape(128, 128)
+                at = b * TILE + u * 128
+                ht[t * 128 : (t + 1) * 128, at : at + 128] = piece.T.astype(BF16)
 
     @pl.loop(0, NG + 1)
     def _(i):
@@ -447,9 +423,9 @@
     await_bytes(v1.at[pl.ds(0, 16)], first.at[NG - 1])
     await_bytes(rs.at[pl.ds(0, 3), :, 0], snd.at[1])
     await_bytes(rs.at[pl.ds(0, 2)], snd.at[2])
-    await_bytes(s3a.at[n63], snd.at[4])
-    await_bytes(s3b.at[n63], snd.at[8])
-    await_bytes(s3b.at[n63], snd.at[9])
+    await_bytes(r2.at[2, n63], away.at[2])
+    for b in range(3):
+        await_bytes(s3.at[b, n63], back.at[b])
     await_bytes(rs.at[pl.ds(0, 2)], snd.at[5])
     await_bytes(zr, snd.at[6])
     await_bytes(r4.at[pl.ds(0, 62)], snd.at[7])
@@ -481,14 +457,10 @@
             pltpu.VMEM((4, NG, 2, 8, *chunk), BF16),
             pltpu.VMEM((768, 256), BF16),
             pltpu.VMEM((3, 512, 256), F32),
-            pltpu.VMEM((2, 32, 16, 128), BF16),
-            pltpu.VMEM((2, 32, 8, 128), BF16),
-            pltpu.VMEM((64, 16, 128), BF16),
-            pltpu.VMEM((64, 8, 128), BF16),
-            pltpu.VMEM((64, 16, 128), BF16),
-            pltpu.VMEM((64, 8, 128), BF16),
-            pltpu.VMEM((2, 32, 16, 128), BF16),
-            pltpu.VMEM((2, 32, 8, 128), BF16),
+            pltpu.VMEM((3, 2, 32, 8, 128), BF16),
+            pltpu.VMEM((3, 64, 8, 128), BF16),
+            pltpu.VMEM((3, 64, 8, 128), BF16),
+            pltpu.VMEM((3, 2, 32, 8, 128), BF16),
             pltpu.VMEM((256, 768), BF16),
             pltpu.VMEM((768, 256), F32),
             pltpu.VMEM((4, NG, 2, 8, *chunk), BF16),
@@ -497,8 +469,8 @@
             pltpu.VMEM((3, NG, 8, *chunk), BF16),
             pltpu.VMEM((2, NG, 8, *chunk), BF16),
             pltpu.VMEM((64, *chunk), BF16),
-            dma((5,)), dma, dma, dma((10,)), dma((NG,)), dma((NG,)), dma((NG,)), dma((3, NG)), dma((4, NG)),
-            dma((2,)), dma((2,)), dma((2, NG)), dma((3, NG)), dma,
+            dma((5,)), dma, dma, dma((8,)), dma((NG,)), dma((3,)), dma((3,)), dma((NG,)), dma((NG,)), dma((3, NG)), dma((4, NG)),
+            dma((3,)), dma((3,)), dma((2, NG)), dma((3, NG)), dma,
         ],
         compiler_params=pltpu.CompilerParams(
             collective_id=0, has_side_effects=True, vmem_limit_bytes=50 * 1024 * 1024

time: 80.2 us -> 78.1 us (0.974)
  Pallas kernels: 78.9 us -> 76.9 us
    pallas_call x1, Pallas kernels: 78.9 us -> 76.9 us  [focus_update(): pl.pallas_call(focus_kernel, out_shape=pltpu.VMEM((1536, 512), BF16), in_...]
where the time goes in v5:
time: 78.1 us; the launch traced here: 78 us
  Pallas kernels  76.9 us (98%)
  local copies, waits for them, and re-layouts  1.15 us (1%)
    pallas_call x1, Pallas kernels, focus_update(): pl.pallas_call(focus_kernel, out_shape=pltpu.VMEM((1536, 512), BF16), in_...  76.9 us

profile of v5, /device:TPU:1, one launch (start us, length us, event | category | flops | bytes accessed | tf_op | source)
XLA Modules:
  0.0 78.0 jit_solution(7605436833962815133)
XLA Ops:
  0.0 76.9 %focus_update.1 = bf16[1536,512]{1,0:T(8,128)(2,1)S(1)} custom-call(bf16[1536,512]{1,0:T(8,128)(2,1)} %bitcast.6, bf16[2,768,3072]{2,1,0:T(8,128)(2,1)} %bitcast.5, s32[12,12]{1,0:T(8,128)} %mask_ref.1, s32[1,128]{1,0:T(1,128)} %bitcast.7, s32[128]{0:T(128)} %onset_smem.1, bf16[512,128]{1,0:T(8,128)(2,1)} %constant.8.fwd_hbm, ...), custom_call_target="tpu_custom_call" | custom-call | tf_op jit(solution)/shard_map/focus_update/pallas_call | solution.py:440
  76.9 1.1 %copy.8 = bf16[32,48,512]{2,1,0:T(8,128)(2,1)} copy(bf16[32,48,512]{2,1,0:T(8,128)(2,1)S(1)} %bitcast.4) | data formatting | bytes 3145728

commit v6 on v5

--- a/solution.py
+++ b/solution.py
@@ -59,9 +59,9 @@
 
 
 def focus_kernel(
-    focus_hbm, kern_hbm, mask_ref, onset_hbm, onset_smem, fwd_hbm, fwdt_hbm, inv_hbm, invt_hbm,
+    focus_hbm, kern_hbm, mask_hbm, onset_hbm, scalar_hbm, fwd_hbm, fwdt_hbm, inv_hbm, invt_hbm,
     out_ref,
-    onset_ref, fwd_ref, fwdt_ref, inv_ref, invt_ref, xv, mv, big, tr, v1, b1, r1, fv, acc, s2, r2, s3, h3, ht, pv, rs, qv, zs, zr, s4, r4,
+    mask_ref, onset_smem, onset_ref, fwd_ref, fwdt_ref, inv_ref, invt_ref, xv, mv, big, tr, v1, b1, r1, fv, acc, s2, r2, s3, h3, ht, pv, rs, qv, zs, zr, s4, r4,
     sem_t, sem_x, sem_m, snd, first, away, back, rcva, rcvb, rel, chip, rcv2, rcv3, rcvq, rcvz, rcv4,
 ):
     me = lax.axis_index("wide")
@@ -97,6 +97,7 @@
             (
                 (fwd_hbm, fwd_ref), (fwdt_hbm, fwdt_ref), (inv_hbm, inv_ref),
                 (invt_hbm, invt_ref), (onset_hbm, onset_ref),
+                (mask_hbm, mask_ref), (scalar_hbm, onset_smem),
             )
         )
     ]
@@ -153,6 +154,8 @@
             send(v1.at[k + 1 - yl], b1.at[here], first.at[i], rcvb.at[x], peer, hf)
 
         if i == 0:
+            for table in tables[1:]:
+                table.wait()
             copy_m.wait()
         if i < 3:
 
@@ -169,8 +172,6 @@
         if i >= 1:
             await_bytes(v1.at[pl.ds(0, 14 if i == 1 else 16)], first.at[i - 1])
 
-    for table in tables[1:]:
-        table.wait()
     acc[...] = jnp.zeros_like(acc)
     sign = jnp.where(low64, -1.0, 1.0).astype(F32)
 
@@ -435,14 +436,15 @@
     dma = pltpu.SemaphoreType.DMA
     vmem = pl.BlockSpec(memory_space=pltpu.VMEM)
     hbm = pl.BlockSpec(memory_space=pl.ANY)
-    smem = pl.BlockSpec(memory_space=pltpu.SMEM)
     chunk = (CH, 128)
     return pl.pallas_call(
         focus_kernel,
         out_shape=pltpu.VMEM((1536, 512), BF16),
-        in_specs=[hbm, hbm, smem, hbm, smem, hbm, hbm, hbm, hbm],
+        in_specs=[hbm, hbm, hbm, hbm, hbm, hbm, hbm, hbm, hbm],
         out_specs=vmem,
         scratch_shapes=[
+            pltpu.SMEM((12, 12), jnp.int32),
+            pltpu.SMEM((128,), jnp.int32),
             pltpu.VMEM((1, 128), jnp.int32),
             pltpu.VMEM((512, 128), BF16),
             pltpu.VMEM((128, 512), BF16),
@@ -469,7 +471,7 @@
             pltpu.VMEM((3, NG, 8, *chunk), BF16),
             pltpu.VMEM((2, NG, 8, *chunk), BF16),
             pltpu.VMEM((64, *chunk), BF16),
-            dma((5,)), dma, dma, dma((8,)), dma((NG,)), dma((3,)), dma((3,)), dma((NG,)), dma((NG,)), dma((3, NG)), dma((4, NG)),
+            dma((7,)), dma, dma, dma((8,)), dma((NG,)), dma((3,)), dma((3,)), dma((NG,)), dma((NG,)), dma((3, NG)), dma((4, NG)),
             dma((3,)), dma((3,)), dma((2, NG)), dma((3, NG)), dma,
         ],
         compiler_params=pltpu.CompilerParams(
@@ -485,7 +487,7 @@
     pinned = functools.partial(pltpu.with_memory_space_constraint, memory_space=pltpu.HBM)
     out = focus_update(
         pinned(focus.reshape(own_points * local_receivers, length)),
-        pinned(kernel[0]), pinned(tile_mask), pinned(onset.reshape(1, 128)), onset, *map(pinned, (fwd, fwdt, inv, invt)),
+        pinned(kernel[0]), pinned(tile_mask), pinned(onset.reshape(1, 128)), pinned(onset), *map(pinned, (fwd, fwdt, inv, invt)),
     )
     return out.reshape(focus.shape)
 

time: 78.1 us -> 77.1 us (0.987)
  Pallas kernels: 76.9 us -> 75.9 us
    pallas_call x1, Pallas kernels: 76.9 us -> 75.9 us  [focus_update(): pl.pallas_call(focus_kernel, out_shape=pltpu.VMEM((1536, 512), BF16), in_...]
where the time goes in v6:
time: 77.1 us
  Pallas kernels  75.9 us (98%)
  local copies, waits for them, and re-layouts  1.15 us (1%)
    pallas_call x1, Pallas kernels, focus_update(): pl.pallas_call(focus_kernel, out_shape=pltpu.VMEM((1536, 512), BF16), in_...  75.9 us

profile of v6, /device:TPU:1, one launch (start us, length us, event | category | flops | bytes accessed | tf_op | source)
XLA Modules:
  0.0 77.1 jit_solution(2845979902203184316)
XLA Ops:
  0.0 75.9 %focus_update.1 = bf16[1536,512]{1,0:T(8,128)(2,1)S(1)} custom-call(bf16[1536,512]{1,0:T(8,128)(2,1)} %bitcast.6, bf16[2,768,3072]{2,1,0:T(8,128)(2,1)} %bitcast.5, s32[12,12]{1,0:T(8,128)} %mask_hbm.1, s32[1,128]{1,0:T(1,128)} %bitcast.7, s32[128]{0:T(128)} %scalar_hbm.1, bf16[512,128]{1,0:T(8,128)(2,1)} %constant.8.fwd_hbm, ...), custom_call_target="tpu_custom_call" | custom-call | tf_op jit(solution)/shard_map/focus_update/pallas_call | solution.py:440
  75.9 1.1 %copy.8 = bf16[32,48,512]{2,1,0:T(8,128)(2,1)} copy(bf16[32,48,512]{2,1,0:T(8,128)(2,1)S(1)} %bitcast.4) | data formatting | bytes 3145728
